TPU v7x, 32 devices: a whole 2x2x4 slice. The times are simulated.
32 devices in a mesh: shard: 4 (over y, core), rep: 8 (over z, x).
Axes of the slice: x: 2, y: 2, z: 4, core: 2. Of those that a mesh axis runs over, the one named last changes fastest.
Arguments:
- tokens: bfloat16 [8, 512, 768], P('rep', 'shard'), may hold values from -6 to 6
- gain_one: bfloat16 [768], P('shard'), may hold values from 0.5 to 1.5
- qkv_weight: bfloat16 [768, 2304], P('shard'), may hold values from -6 to 6
- out_weight: bfloat16 [768, 768], P('shard'), may hold values from -2.5 to 2.5
- gain_two: bfloat16 [768], P('shard'), may hold values from 0.5 to 1.5
- in_weight: bfloat16 [768, 2304], P('shard'), may hold values from -0.21875 to 0.21875
- down_weight: bfloat16 [1152, 768], P('shard'), may hold values from -0.1875 to 0.1875
- grad_output: bfloat16 [8, 512, 768], P('rep', 'shard'), may hold values from -6 to 6
Outputs:
- output: bfloat16 [8, 512, 768], P('rep', 'shard')
- grad_tokens: float32 [8, 512, 768], P('rep', 'shard')
- grad_gain_one: float32 [768], P('shard')
- grad_qkv: float32 [768, 2304], P('shard')
- grad_out: float32 [768, 768], P('shard')
- grad_gain_two: float32 [768], P('shard')
- grad_in: float32 [768, 2304], P('shard')
- grad_down: float32 [1152, 768], P('shard')
All inputs are finite; a program needn't handle non-finite values.
Results may differ from a plain program's by a relative error of at most 0.02.
Values may be sent and summed in bfloat16 or wider, within the bound.
A program may use at most 128 MiB of HBM per device.

v0:
```python
import functools

import jax
import jax.numpy as jnp
from jax import lax
from jax.experimental import pallas as pl
from jax.experimental.pallas import tpu as pltpu
from jax.sharding import PartitionSpec as P

HEAD_DIM = 64
EPSILON = 1e-05
THETA = 160000.0
SQRT_HALF = 0.7071067811865476
INV_SQRT_TAU = 0.3989422804014327
MESH_ID = pl.DeviceIdType.MESH
LANES = 128
VMEM = pl.BlockSpec(memory_space=pltpu.VMEM)


def layer_norm(values, gain):
    mean_row = jnp.mean(values, axis=-1, keepdims=True)
    centred = values - mean_row
    variance = jnp.mean(centred * centred, axis=-1, keepdims=True)
    inverse = lax.rsqrt(variance + EPSILON)
    normed = centred * inverse
    return (normed, inverse, normed * gain.astype(jnp.float32))


def norm_backward(grad_out, normed, inverse, gain):
    grad_normed = grad_out * gain.astype(jnp.float32)
    gain_grad = jnp.sum(grad_out * normed, axis=0)
    first = jnp.mean(grad_normed, axis=-1, keepdims=True)
    second = jnp.mean(grad_normed * normed, axis=-1, keepdims=True)
    return (inverse * (grad_normed - first - normed * second), gain_grad)


def rotary_tables(count, head_dim):
    half = head_dim // 2
    positions = jnp.arange(count, dtype=jnp.int32)
    freq = THETA ** (-jnp.arange(half, dtype=jnp.float32) * 2.0 / head_dim)
    angles = positions.astype(jnp.float32)[:, None] * freq[None, :]
    angles = jnp.concatenate([angles, angles], axis=-1)
    return (jnp.cos(angles)[None], jnp.sin(angles)[None])


def rotate_half(values):
    half = values.shape[-1] // 2
    return jnp.concatenate([-values[..., half:], values[..., :half]], axis=-1)


def gelu_pair(inner):
    cdf = 0.5 * (1.0 + jax.scipy.special.erf(inner * SQRT_HALF))
    return (inner * cdf, cdf + inner * jnp.exp(-0.5 * inner * inner) * INV_SQRT_TAU)


def outer_sum(left, right):
    return lax.dot_general(
        left, right, (((0,), (0,)), ((), ())), preferred_element_type=jnp.float32
    )


def times_transposed(left, weight):
    return lax.dot_general(
        left, weight, (((1,), (1,)), ((), ())), preferred_element_type=jnp.float32
    )


def flip(index, bit):
    return index + bit * (1 - 2 * ((index // bit) % 2))


def remote(src, dst, send, recv, axis, target):
    return pltpu.make_async_remote_copy(
        src_ref=src,
        dst_ref=dst,
        send_sem=send,
        recv_sem=recv,
        device_id={axis: target},
        device_id_type=MESH_ID,
    )


def greet(partners):
    barrier = pltpu.get_barrier_semaphore()
    for axis, target in partners:
        pl.semaphore_signal(barrier, inc=1, device_id={axis: target}, device_id_type=MESH_ID)
    pl.semaphore_wait(barrier, len(partners))


def shard_partners(me):
    return [("shard", flip(me, 1)), ("shard", flip(me, 2)), ("shard", flip(flip(me, 1), 2))]


def gather_kernel(gathered, kinds, relays, *refs):
    total = gathered + len(kinds)
    ins, outs = refs[:total], refs[total : 2 * total]
    packed = refs[2 * total : 2 * total + len(kinds)]
    send, recv, local_sem = refs[2 * total + len(kinds) :]
    me = lax.axis_index("shard")
    partners = shard_partners(me)
    rep = lax.axis_index("rep")
    bits = [1 << b for b in range(relays)] if kinds else []
    greet(partners + [("rep", flip(rep, bit)) for bit in bits])
    (_, core), (_, chip), (_, diagonal) = partners
    pending = []

    def begin(i):
        far = remote(ins[i], outs[i].at[me], send.at[i, 0], recv.at[i, 0], "shard", chip)
        far.start()
        near = remote(ins[i], outs[i].at[me], send.at[i, 1], recv.at[i, 1], "shard", core)
        near.start()
        own = pltpu.make_async_copy(ins[i], outs[i].at[me], local_sem.at[i])
        own.start()
        pending.append((far, near, own))

    def pass_on(i):
        pending[i][0].wait_recv()
        relay = remote(
            outs[i].at[chip], outs[i].at[chip], send.at[i, 2], recv.at[i, 2], "shard", core
        )
        relay.start()
        pending[i] = pending[i] + (relay,)

    late = gathered - 1 if kinds else gathered
    for i in range(late):
        begin(i)
    shared, whole_copies, own_copies = [], [], []
    for i in range(gathered, total):
        source, buffer, kind_count = ins[i], packed[i - gathered], kinds[i - gathered]
        blocks, tall, columns = buffer.shape
        size = columns // kind_count
        for j in range(blocks):
            for kind in range(kind_count):
                start = (kind * blocks + j) * size
                buffer[j, :, kind * size : (kind + 1) * size] = source[:, start : start + size]
        share = tall >> relays
        rows = pl.ds(pl.multiple_of((rep % (1 << relays)) * share, share), share)
        for k, target in enumerate((chip, diagonal)):
            copy = remote(
                buffer.at[target, rows],
                outs[i].at[me, rows],
                send.at[i, k],
                recv.at[i, k],
                "shard",
                target,
            )
            copy.start()
            shared.append((i, k, target, tall, [copy]))
        copy = remote(
            buffer.at[core], outs[i].at[me], send.at[i, 2], recv.at[i, 2], "shard", core
        )
        copy.start()
        whole_copies.append(copy)
        own = pltpu.make_async_copy(buffer.at[me], outs[i].at[me], local_sem.at[i])
        own.start()
        own_copies.append(own)
    for i in range(late, gathered):
        begin(i)
    for i in range(late):
        pass_on(i)
    for level, bit in enumerate(bits):
        for i, k, target, tall, copies in shared:
            copies[-1].wait_recv()
            length = (tall >> relays) * bit
            first = ((rep % (1 << relays)) // bit) * length
            region = outs[i].at[target, pl.ds(pl.multiple_of(first, length), length)]
            slot = 3 + 2 * level + k
            copy = remote(
                region, region, send.at[i, slot], recv.at[i, slot], "rep", flip(rep, bit)
            )
            copy.start()
            copies.append(copy)
    for i in range(late, gathered):
        pass_on(i)
    for _, _, _, _, copies in shared:
        copies[-1].wait_recv()
        for copy in copies:
            copy.wait_send()
    for far, near, own, relay in pending:
        far.wait_send()
        near.wait()
        own.wait()
        relay.wait()
    for copy in whole_copies + own_copies:
        copy.wait()


def gather(collective, gathered, swapped, kinds, n_shard, n_rep=1):
    arrays = tuple(gathered) + tuple(swapped)
    shapes = [jax.ShapeDtypeStruct((n_shard,) + a.shape, a.dtype) for a in gathered]
    blocks = [
        jax.ShapeDtypeStruct((n_shard, a.shape[0], a.shape[1] // n_shard), a.dtype)
        for a in swapped
    ]
    relays = 0
    if swapped:
        relays = min(2, n_rep.bit_length() - 1)
        while relays and any(a.shape[0] % (16 << relays) for a in swapped):
            relays -= 1
    return pl.pallas_call(
        functools.partial(gather_kernel, len(gathered), tuple(kinds), relays),
        out_shape=tuple(shapes + blocks),
        in_specs=[VMEM] * len(arrays),
        out_specs=tuple([VMEM] * len(arrays)),
        scratch_shapes=[pltpu.VMEM(b.shape, b.dtype) for b in blocks]
        + [
            pltpu.SemaphoreType.DMA((len(arrays), 3 + 2 * relays)),
            pltpu.SemaphoreType.DMA((len(arrays), 3 + 2 * relays)),
            pltpu.SemaphoreType.DMA((len(arrays),)),
        ],
        compiler_params=pltpu.CompilerParams(collective_id=collective, has_side_effects=True),
    )(*arrays)


def scatter_kernel(total, *refs):
    ins, outs = refs[:total], refs[total : 2 * total]
    near_buf, out_buf, far_buf, send, recv = refs[2 * total :]
    me = lax.axis_index("shard")
    partners = shard_partners(me)[:2]
    greet(partners)
    (_, core), (_, chip) = partners
    diagonal = flip(core, 2)
    first, second, third = [], [], []
    for i in range(total):
        a = remote(
            ins[i].at[diagonal], near_buf.at[i, 0], send.at[i, 0], recv.at[i, 0], "shard", core
        )
        a.start()
        b = remote(ins[i].at[core], near_buf.at[i, 1], send.at[i, 1], recv.at[i, 1], "shard", core)
        b.start()
        first.append(a)
        second.append(b)
    for i in range(total):
        first[i].wait_recv()
        out_buf[i] = (
            ins[i][chip].astype(jnp.float32) + near_buf[i, 0].astype(jnp.float32)
        ).astype(jnp.bfloat16)
        c = remote(out_buf.at[i], far_buf.at[i], send.at[i, 2], recv.at[i, 2], "shard", chip)
        c.start()
        third.append(c)
    for i in range(total):
        second[i].wait_recv()
        outs[i][...] = ins[i][me].astype(jnp.float32) + near_buf[i, 1].astype(jnp.float32)
    for i in range(total):
        third[i].wait_recv()
        outs[i][...] += far_buf[i].astype(jnp.float32)
    for i in range(total):
        first[i].wait_send()
        second[i].wait_send()
        third[i].wait_send()


def scatter(collective, arrays):
    total = len(arrays)
    block = arrays[0].shape[1:]
    return pl.pallas_call(
        functools.partial(scatter_kernel, total),
        out_shape=tuple([jax.ShapeDtypeStruct(block, jnp.float32)] * total),
        in_specs=[VMEM] * total,
        out_specs=tuple([VMEM] * total),
        scratch_shapes=[
            pltpu.VMEM((total, 2) + block, jnp.bfloat16),
            pltpu.VMEM((total,) + block, jnp.bfloat16),
            pltpu.VMEM((total,) + block, jnp.bfloat16),
            pltpu.SemaphoreType.DMA((total, 3)),
            pltpu.SemaphoreType.DMA((total, 3)),
        ],
        compiler_params=pltpu.CompilerParams(collective_id=collective, has_side_effects=True),
    )(*arrays)


def halves(order, me):
    length = 1 << len(order)
    offset = 0
    plan = []
    for bit in order:
        length //= 2
        side = (me // bit) % 2
        plan.append((bit, offset + side * length, offset + (1 - side) * length, length))
        offset = offset + side * length
    return plan


class Stream:
    def __init__(self, buffer, base, rows, order, swap):
        self.buffer, self.base, self.rows, self.order, self.swap = buffer, base, rows, order, swap


def streams_of(buffer, rows, n_rep, swap):
    tiles = -(-rows // (16 * n_rep))
    low_first = tuple(1 << i for i in range(n_rep.bit_length() - 1))
    orders = (low_first, low_first[1::-1] + low_first[2:])
    streams = []
    base = 0
    for share, order in zip((tiles - tiles // 2, tiles // 2), orders):
        if share:
            streams.append(Stream(buffer, base, 16 * share, order, swap))
            base += 16 * share * n_rep
    return streams, base


class RepSum:
    def __init__(self, streams, acc, box, res, sems):
        self.streams, self.acc, self.box, self.res = streams, acc, box, res
        self.send, self.recv, self.swap_send, self.swap_recv, self.local_sem = sems
        self.rep = lax.axis_index("rep")
        self.me = lax.axis_index("shard")
        self.group = shard_partners(self.me)
        self.steps = len(streams[0].order)
        self.plans = [halves(stream.order, self.rep) for stream in streams]
        self.started = [[] for _ in streams]

    def at(self, ref, i, piece, length, lead=None):
        stream = self.streams[i]
        start = stream.base + piece * stream.rows
        if not isinstance(start, int):
            start = pl.multiple_of(start, 16)
        rows = pl.ds(start, length * stream.rows)
        if not stream.swap:
            return ref.at[rows]
        return ref.at[slice(None) if lead is None else lead, rows]

    def begin(self, i, k):
        stream, plan, steps = self.streams[i], self.plans[i], self.steps
        acc, box, res = (refs[stream.buffer] for refs in (self.acc, self.box, self.res))
        if k < steps:
            bit, _, sent, length = plan[k]
            copies = [
                remote(
                    self.at(acc, i, sent, length),
                    self.at(box, i, length, length),
                    self.send.at[i, k],
                    self.recv.at[i, k],
                    "rep",
                    flip(self.rep, bit),
                )
            ]
        elif k == steps:
            mine = plan[-1][1]
            if not stream.swap:
                copies = [
                    pltpu.make_async_copy(
                        self.at(acc, i, mine, 1), self.at(res, i, mine, 1), self.local_sem.at[i]
                    )
                ]
            else:
                target_block = self.at(res, i, mine, 1, self.me)
                copies = [
                    remote(
                        self.at(acc, i, mine, 1, target),
                        target_block,
                        self.swap_send.at[i, j],
                        self.swap_recv.at[i, j],
                        "shard",
                        target,
                    )
                    for j, (_, target) in enumerate(self.group)
                ]
                copies.append(
                    pltpu.make_async_copy(
                        self.at(acc, i, mine, 1, self.me), target_block, self.local_sem.at[i]
                    )
                )
        else:
            bit, kept, _, length = plan[2 * steps - k]
            region = self.at(res, i, kept, length)
            copies = [
                remote(
                    region,
                    region,
                    self.send.at[i, k - 1],
                    self.recv.at[i, k - 1],
                    "rep",
                    flip(self.rep, bit),
                )
            ]
        for copy in copies:
            copy.start()
        self.started[i].append(copies)

    def finish(self, i, k):
        copies, stream = self.started[i][k], self.streams[i]
        if k == self.steps:
            for copy in copies:
                copy.wait()
            return
        copies[0].wait_recv()
        if k > self.steps:
            return
        acc, box = self.acc[stream.buffer], self.box[stream.buffer]
        _, kept, _, length = self.plans[i][k]
        blocks = range(acc.shape[0]) if stream.swap else (None,)

        @pl.loop(0, length)
        def _(p):
            to = pl.multiple_of(stream.base + (kept + p) * stream.rows, 16)
            of = pl.multiple_of(stream.base + (length + p) * stream.rows, 16)
            to, of = pl.ds(to, stream.rows), pl.ds(of, stream.rows)
            for block in blocks:
                x, y = ((to,), (of,)) if block is None else ((block, to), (block, of))
                acc[x] = (acc[x].astype(jnp.float32) + box[y].astype(jnp.float32)).astype(
                    jnp.bfloat16
                )

    def begin_all(self, chosen):
        for i in chosen:
            self.begin(i, 0)

    def step(self, i, k):
        self.finish(i, k)
        if k < 2 * self.steps:
            self.begin(i, k + 1)

    def close(self, chosen):
        for i in chosen:
            for k in range(2 * self.steps + 1):
                if k != self.steps:
                    self.started[i][k][0].wait_send()


def pack_columns(source, target, gain):
    blocks, rows, columns = source.shape
    full, rest = divmod(columns, LANES)
    for s in range(blocks):
        for j in range(full):
            target[s, j * rows : (j + 1) * rows] = source[s, :, j * LANES : (j + 1) * LANES]
        at = full * rows
        if rest:
            half = rows // 2
            target[s, at : at + half, :rest] = source[s, :half, full * LANES :]
            target[s, at : at + half, rest:] = source[s, half:, full * LANES :]
            at += half
        if gain is not None:
            target[s, at : at + 16] = gain[s]
            at += 16
        if at < target.shape[1]:
            target[s, at:] = jnp.zeros((target.shape[1] - at, LANES), target.dtype)


def pack_gain(gain, target, at):
    blocks = target.shape[0]
    part = gain.shape[1] // blocks
    row = lax.broadcasted_iota(jnp.int32, (16, LANES), 0)
    for s in range(blocks):
        tile = jnp.zeros((16, LANES), jnp.float32)
        for j in range(-(-part // LANES)):
            piece = gain[:, s * part + j * LANES : s * part + min((j + 1) * LANES, part)]
            room = LANES - piece.shape[1]
            if room:
                piece = jnp.concatenate([piece, jnp.zeros((1, room), jnp.float32)], axis=1)
            tile = jnp.where(row == j, jnp.broadcast_to(piece, (16, LANES)), tile)
        target[s, at : at + 16] = tile.astype(target.dtype)


def unpack_columns(source, out, gain_out, kinds):
    blocks = source.shape[0]
    rows, width = out.shape
    columns = width // blocks
    size = columns // kinds
    full, rest = divmod(columns, LANES)
    half = rows // 2
    at = full * rows
    gain = jnp.zeros((16, LANES), jnp.float32)
    for t in range(blocks):
        parts = [source[t, j * rows : (j + 1) * rows] for j in range(full)]
        end = at
        if rest:
            tail = source[t, at : at + half]
            parts.append(jnp.concatenate([tail[:, :rest], tail[:, rest:]], axis=0))
            end += half
        block = jnp.concatenate(parts, axis=1)
        gain += source[t, end : end + 16].astype(jnp.float32)
        for kind in range(kinds):
            start = (kind * blocks + t) * size
            out[:, start : start + size] = block[:, kind * size : (kind + 1) * size]
    gain_out[...] = gain


def pack_rows(sources, target):
    tall = sum(source.shape[0] for source in sources)
    at = 0
    for source in sources:
        rows = source.shape[0]
        for j in range(source.shape[1] // LANES):
            target[j * tall + at : j * tall + at + rows] = source[:, j * LANES : (j + 1) * LANES]
        at += rows
    end = tall * sources[0].shape[1] // LANES
    if end < target.shape[0]:
        target[end:] = jnp.zeros((target.shape[0] - end, LANES), target.dtype)


def unpack_rows(source, outs):
    tall = sum(out.shape[0] for out in outs)
    at = 0
    for out in outs:
        rows = out.shape[0]
        for j in range(out.shape[1] // LANES):
            out[:, j * LANES : (j + 1) * LANES] = source[
                j * tall + at : j * tall + at + rows
            ]
        at += rows


def column_rows(shape):
    _, rows, columns = shape
    return rows * columns // LANES + 16


def sum_kernel(streams, early, qkv, h1_part, normed, win, gain2, gout, gdown, *refs):
    o_qkv, o_gain1, o_in, o_gain2, o_out, o_down, o_h1 = refs[:7]
    acc, box, res = refs[7:10], refs[10:13], refs[13:16]
    near_buf, out_buf, far_buf, h1_send, h1_recv = refs[16:21]
    rep_sum = RepSum(streams, acc, box, res, refs[21:])
    me = rep_sum.me
    core, chip = flip(me, 1), flip(me, 2)
    bits = sorted(streams[0].order)
    greet([("rep", flip(rep_sum.rep, bit)) for bit in bits] + rep_sum.group)
    first = [
        remote(
            h1_part.at[target], near_buf.at[j], h1_send.at[j], h1_recv.at[j], "shard", core
        )
        for j, target in enumerate((flip(core, 2), core))
    ]
    for copy in first:
        copy.start()
    pack_rows((gout, gdown), acc[0])
    pack_columns(win, acc[1], gain2)
    rep_sum.begin_all(range(early))
    first[0].wait_recv()
    out_buf[...] = (
        h1_part[chip].astype(jnp.float32) + near_buf[0].astype(jnp.float32)
    ).astype(jnp.bfloat16)
    last = remote(out_buf, far_buf, h1_send.at[2], h1_recv.at[2], "shard", chip)
    last.start()
    pack_columns(qkv, acc[2], None)
    first[1].wait_recv()
    own = h1_part[me].astype(jnp.float32) + near_buf[1].astype(jnp.float32)
    last.wait_recv()
    grad_h1 = own + far_buf[...].astype(jnp.float32)
    o_h1[...] = grad_h1
    gain = jnp.sum(grad_h1 * normed[...], axis=0, keepdims=True)
    pack_gain(gain, acc[2], column_rows(qkv.shape) - 16)
    rep_sum.begin_all(range(early, len(streams)))
    pairs = len(streams) // 2
    for t in range(2 * rep_sum.steps + 1 + pairs):
        for i in range(len(streams)):
            k = t - i // 2
            if 0 <= k <= 2 * rep_sum.steps:
                rep_sum.step(i, k)
    for copy in first + [last]:
        copy.wait_send()
    unpack_rows(res[0], (o_out, o_down))
    unpack_columns(res[1], o_in, o_gain2, 2)
    unpack_columns(res[2], o_qkv, o_gain1, 3)
    rep_sum.close(range(len(streams)))


def sum_over_rep(collective, n_rep, qkv, h1_part, normed, win, gain2, gout, gdown):
    b16, f32 = jnp.bfloat16, jnp.float32
    n_shard, part, columns = qkv.shape
    width = columns * n_shard
    plain_rows = (gout.shape[0] + gdown.shape[0]) * gout.shape[1] // LANES
    streams, shapes, early = [], [], 0
    for i, (rows, swap) in enumerate(
        ((plain_rows, False), (column_rows(win.shape), True), (column_rows(qkv.shape), True))
    ):
        more, padded = streams_of(i, rows, n_rep, swap)
        early = len(streams)
        streams += more
        shapes.append((n_shard, padded, LANES) if swap else (padded, LANES))
    steps = len(streams[0].order)
    count = len(streams)
    outs = [(part, width), (16, LANES), (part, win.shape[2] * n_shard), (16, LANES)]
    outs += [gout.shape, gdown.shape, normed.shape]
    wide = ((16, LANES), normed.shape)
    return pl.pallas_call(
        functools.partial(sum_kernel, streams, early),
        out_shape=tuple(
            jax.ShapeDtypeStruct(shape, f32 if shape in wide else b16) for shape in outs
        ),
        in_specs=[VMEM] * 7,
        out_specs=tuple([VMEM] * 7),
        scratch_shapes=[pltpu.VMEM(shape, b16) for shape in shapes * 3]
        + [
            pltpu.VMEM((2,) + normed.shape, b16),
            pltpu.VMEM(normed.shape, b16),
            pltpu.VMEM(normed.shape, b16),
            pltpu.SemaphoreType.DMA((3,)),
            pltpu.SemaphoreType.DMA((3,)),
            pltpu.SemaphoreType.DMA((count, 2 * steps)),
            pltpu.SemaphoreType.DMA((count, 2 * steps)),
            pltpu.SemaphoreType.DMA((count, 3)),
            pltpu.SemaphoreType.DMA((count, 3)),
            pltpu.SemaphoreType.DMA((count,)),
        ],
        compiler_params=pltpu.CompilerParams(collective_id=collective, has_side_effects=True),
    )(qkv, h1_part, normed, win, gain2, gout, gdown)


def local(
    n_shard, n_rep, tokens, gain_one, qkv_weight, out_weight, gain_two, in_weight, down_weight,
    grad_output
):
    tok_dev, width = tokens.shape[1:]
    part = width // n_shard
    heads = part // HEAD_DIM
    hidden = down_weight.shape[0]
    count = tok_dev * n_shard
    scale = HEAD_DIM ** (-0.5)
    f32, b16 = jnp.float32, jnp.bfloat16
    own_tokens = tokens.reshape(tok_dev, width)
    own_grad = grad_output.reshape(tok_dev, width)

    all_tokens, all_g1, all_g2, all_grad, my_qkv, my_in = gather(
        0,
        (own_tokens, gain_one.reshape(1, part), gain_two.reshape(1, part), own_grad),
        (qkv_weight, in_weight),
        (3, 2),
        n_shard,
        n_rep,
    )
    full_g1 = all_g1.reshape(width)
    full_g2 = all_g2.reshape(width)
    my_qkv = my_qkv.reshape(width, 3 * part)
    my_in = my_in.reshape(width, 2 * hidden)
    grad_b = all_grad.reshape(count, width)

    inputs = own_tokens.astype(f32)
    normed_one, inverse_one, _ = layer_norm(inputs, full_g1)
    hidden_one = layer_norm(all_tokens.reshape(count, width).astype(f32), full_g1)[2].astype(b16)
    projected = jnp.dot(hidden_one, my_qkv, preferred_element_type=f32)
    cosine, sine = rotary_tables(count, HEAD_DIM)
    split = projected.reshape(count, 3, heads, HEAD_DIM).transpose(1, 2, 0, 3)
    queries, key_raw = split[0], split[1]
    query_rot = (queries * cosine + rotate_half(queries) * sine).astype(b16)
    key_rot = (key_raw * cosine + rotate_half(key_raw) * sine).astype(b16)
    values = split[2].astype(b16)
    scores = jnp.einsum("hqd,hkd->hqk", query_rot, key_rot, preferred_element_type=f32) * scale
    maxima = jnp.max(scores, axis=-1, keepdims=True)
    expo = jnp.exp(scores - maxima)
    totals = jnp.sum(expo, axis=-1, keepdims=True)
    accum = jnp.einsum("hqk,hkd->hqd", expo.astype(b16), values, preferred_element_type=f32)
    att_heads = (accum / totals).astype(b16)
    attended = att_heads.transpose(1, 0, 2).reshape(count, part)
    partial = jnp.dot(attended, out_weight, preferred_element_type=f32).astype(b16)
    (mixed,) = scatter(1, (partial.reshape(n_shard, tok_dev, width),))
    resid = inputs + mixed
    normed_two, inverse_two, scaled_two = layer_norm(resid, full_g2)
    (hidden_two,) = gather(2, (scaled_two.astype(b16),), (), (), n_shard)
    hidden_two = hidden_two.reshape(count, width)
    upper = jnp.dot(hidden_two, my_in, preferred_element_type=f32)
    inner, gate_half = upper[:, :hidden], upper[:, hidden:]
    gelu_value, gelu_slope = gelu_pair(inner)
    act = (gelu_value * gate_half).astype(b16)
    down_part = jnp.dot(act, down_weight, preferred_element_type=f32).astype(b16)
    grad_down = outer_sum(act, grad_b)
    grad_act = times_transposed(grad_b, down_weight)
    grad_upper = jnp.concatenate(
        [grad_act * gate_half * gelu_slope, grad_act * gelu_value], axis=-1
    ).astype(b16)
    grad_in = outer_sum(hidden_two, grad_upper)
    h2_part = times_transposed(grad_upper, my_in).astype(b16)
    down_sum, grad_h2 = scatter(
        3, (down_part.reshape(n_shard, tok_dev, width), h2_part.reshape(n_shard, tok_dev, width))
    )
    output = (resid + down_sum).astype(b16)
    norm_grad_two, grad_gain_two = norm_backward(grad_h2, normed_two, inverse_two, full_g2)
    grad_resid = own_grad.astype(f32) + norm_grad_two
    (resid_b,) = gather(4, (grad_resid.astype(b16),), (), (), n_shard)
    resid_b = resid_b.reshape(count, width)
    grad_out = outer_sum(attended, resid_b)
    grad_att = times_transposed(resid_b, out_weight).astype(b16)
    grad_heads = grad_att.reshape(count, heads, HEAD_DIM).transpose(1, 0, 2)
    delta = jnp.sum(grad_heads.astype(f32) * att_heads.astype(f32), axis=-1, keepdims=True)
    probs = expo / totals
    grad_value = jnp.einsum(
        "hqk,hqd->khd", probs.astype(b16), grad_heads, preferred_element_type=f32
    )
    grad_probs = jnp.einsum("hqd,hkd->hqk", grad_heads, values, preferred_element_type=f32)
    grad_scores = (probs * (grad_probs - delta) * scale).astype(b16)
    grad_qr = jnp.einsum("hqk,hkd->hqd", grad_scores, key_rot, preferred_element_type=f32)
    grad_kr = jnp.einsum("hqk,hqd->hkd", grad_scores, query_rot, preferred_element_type=f32)
    grad_q = (grad_qr * cosine - rotate_half(grad_qr) * sine).transpose(1, 0, 2)
    grad_k = (grad_kr * cosine - rotate_half(grad_kr) * sine).transpose(1, 0, 2)
    grad_projected = jnp.concatenate(
        [g.reshape(count, part) for g in (grad_q, grad_k, grad_value)], axis=-1
    ).astype(b16)
    grad_qkv = outer_sum(hidden_one, grad_projected)
    h1_part = times_transposed(grad_projected, my_qkv).astype(b16)
    def gain_rows(gain):
        room = -part % LANES
        rows = jnp.pad(gain.reshape(n_shard, part), ((0, 0), (0, room)))
        rows = rows.reshape(n_shard, -1, LANES)
        return jnp.pad(rows, ((0, 0), (0, 16 - rows.shape[1]), (0, 0))).astype(b16)

    sum_qkv, sum_g1, sum_in, sum_g2, sum_out, sum_down, grad_h1 = sum_over_rep(
        6,
        n_rep,
        grad_qkv.astype(b16).reshape(n_shard, part, -1),
        h1_part.reshape(n_shard, tok_dev, width),
        normed_one,
        grad_in.astype(b16).reshape(n_shard, part, -1),
        gain_rows(grad_gain_two),
        grad_out.astype(b16),
        grad_down.astype(b16),
    )
    norm_grad_one, _ = norm_backward(grad_h1, normed_one, inverse_one, full_g1)
    grad_tokens = grad_resid + norm_grad_one
    return (
        output.reshape(1, tok_dev, width),
        grad_tokens.reshape(1, tok_dev, width),
        sum_g1.reshape(-1)[:part],
        sum_qkv.astype(f32),
        sum_out.astype(f32),
        sum_g2.reshape(-1)[:part],
        sum_in.astype(f32),
        sum_down.astype(f32),
    )


def solution(mesh):
    in_specs = (
        P("rep", "shard", None),
        P("shard"),
        P("shard", None),
        P("shard", None),
        P("shard"),
        P("shard", None),
        P("shard", None),
        P("rep", "shard", None),
    )
    out_specs = (
        P("rep", "shard", None),
        P("rep", "shard", None),
        P("shard"),
        P("shard", None),
        P("shard", None),
        P("shard"),
        P("shard", None),
        P("shard", None),
    )
    body = functools.partial(local, mesh.shape["shard"], mesh.shape["rep"])
    return jax.shard_map(body, mesh=mesh, in_specs=in_specs, out_specs=out_specs, check_vma=False)
```

profile of v0, /device:TPU:0, one launch (start us, length us, event | category | flops | bytes accessed | tf_op | source)
XLA Modules:
  0.0 211.5 jit_solution(8531268162590230689)
XLA Ops:
  2.9 1.2 reshape.276.refs_1_
  4.1 1.2 reshape.277.refs_2_
  6.3 32.1 %shard_map.143 = (bf16[4,128,768]{2,1,0:T(8,128)(2,1)}, bf16[4,1,192]{2,1,0:T(2,128)(2,1)}, bf16[4,1,192]{2,1,0:T(2,128)(2,1)}, bf16[4,128,768]{2,1,0:T(8,128)(2...) custom-call(bf16[128,768]{1,0:T(8,128)(2,1)} %bitcast.114, bf16[1,192]{1,0:T(2,128)(2,1)} %reshape.276.refs_1_, ...), custom_call_target="tpu_custom_call" | custom-call | tf_op jit(solution)/shard_map/pallas_call | solution.py:200
  39.3 1.3 convert_reduce_fusion
  40.6 1.5 multiply_reduce_fusion.1
  42.2 1.2 fusion.7
  43.7 1.5 copy.16
  49.4 1.4 fusion.33
  50.8 1.3 convolution_convert_fusion.5
  52.1 10.5 %shard_map.144 = f32[128,768]{1,0:T(8,128)} custom-call(bf16[4,128,768]{2,1,0:T(8,128)(2,1)} %bitcast.118), custom_call_target="tpu_custom_call" | custom-call | tf_op jit(solution)/shard_map/pallas_call | solution.py:256
  62.6 1.9 fusion.49
  65.5 10.2 %shard_map.145 = bf16[4,128,768]{2,1,0:T(8,128)(2,1)} custom-call(bf16[128,768]{1,0:T(8,128)(2,1)} %multiply_convert_fusion.4.refs_0_), custom_call_target="tpu_custom_call" | custom-call | tf_op jit(solution)/shard_map/pallas_call | solution.py:200
  75.7 2.2 %fusion.50 = f32[512,576]{0,1:T(8,128)S(1)} fusion(bf16[512,768]{1,0:T(8,128)(2,1)} %bitcast.120, bf16[768,576]{1,0:T(8,128)(2,1)} %bitcast.126), kind=kOutput, calls=%fused_computation.112 | convolution fusion | flops 452984832 | bytes 2850816 | tf_op jit(solution)/shard_map/dot_general | solution.py:651
  79.7 1.7 convolution_convert_fusion.3
  81.4 1.5 convolution_convert_fusion
  82.9 2.2 %copy.23 = bf16[768,576]{1,0:T(8,128)(2,1)} copy(bf16[768,576]{0,1:T(8,128)(2,1)} %convolution_convert_fusion) | data formatting | bytes 1769472 | tf_op jit(solution)/shard_map/convert_element_type | solution.py:702
  85.2 1.5 convolution_convert_fusion.4
  86.6 15.2 %shard_map.146 = (f32[128,768]{1,0:T(8,128)}, f32[128,768]{1,0:T(8,128)}) custom-call(bf16[4,128,768]{2,1,0:T(8,128)(2,1)} %bitcast.132, bf16[4,128,768]{2,1,0:T(8,128)(2,1)} %bitcast.131), custom_call_target="tpu_custom_call" | custom-call | tf_op jit(solution)/shard_map/pallas_call | solution.py:256
  101.8 1.2 multiply_reduce_fusion.3
  103.2 2.1 fusion.48
  105.9 10.2 %shard_map.147 = bf16[4,128,768]{2,1,0:T(8,128)(2,1)} custom-call(bf16[128,768]{1,0:T(8,128)(2,1)} %get-tuple-element.43.refs_0_), custom_call_target="tpu_custom_call" | custom-call | tf_op jit(solution)/shard_map/pallas_call | solution.py:200
  116.1 2.3 %convolution_convert_fusion.7.gout = bf16[192,768]{1,0:T(8,128)(2,1)} fusion(bf16[512,192]{0,1:T(8,128)(2,1)S(1)} %bitcast.123, bf16[512,768]{1,0:T(8,128)(2,1)} %bitcast.112), kind=kOutput, calls=%fused_computation.26 | convolution fusion | flops 151142400 | bytes 1277952 | tf_op jit(solution)/shard_map/dot_general | solution.py:57
  118.5 1.5 convolution_convert_fusion.8
  124.2 1.7 convolution_convert_fusion.2
  126.5 1.3 copy.22
  127.9 73.2 %shard_map.148 = (bf16[192,2304]{1,0:T(8,128)(2,1)}, f32[16,128]{1,0:T(8,128)}, bf16[192,2304]{1,0:T(8,128)(2,1)}, f32[16,128]{1,0:T(8,128)}, bf16[192,768]{1,0:...) custom-call(bf16[4,192,576]{2,1,0:T(8,128)(2,1)} %bitcast.116, bf16[4,128,768]{2,1,0:T(8,128)(2,1)} %bitcast.136, ...), custom_call_target="tpu_custom_call" | custom-call | tf_op jit(solution)/shard_map/pallas_call | solution.py:576
  201.1 1.3 slice.74
  202.4 1.2 slice.75
  203.6 1.2 multiply_reduce_fusion.7
  204.9 2.0 add_bitcast_fusion
  208.7 1.3 convert_element_type.181
  210.2 1.3 convert_element_type.183
  (86 shorter events, 18.8 us)
Async XLA Ops:
  0.6 77.2 %copy-start = (bf16[288,768]{1,0:T(8,128)(2,1)S(1)}, bf16[288,768]{1,0:T(8,128)(2,1)}, u32[]{:S(2)}) copy-start(bf16[288,768]{1,0:T(8,128)(2,1)} %param.14) | copy-start | bytes 1327108
  6.3 39.8 %copy-start.8 = (f32[512,64]{0,1:T(8,128)}, f32[512,64]{0,1:T(8,128)S(1)}, u32[]{:S(2)}) copy-start(f32[512,64]{0,1:T(8,128)S(1)} %get-tuple-element.66) | copy-start | bytes 393220
  38.5 3.8 %copy-start.3 = (bf16[4,128,768]{2,1,0:T(8,128)(2,1)S(1)}, bf16[4,128,768]{2,1,0:T(8,128)(2,1)}, u32[]{:S(2)}) copy-start(bf16[4,128,768]{2,1,0:T(8,128)(2,1)} %get-tuple-element.23) | copy-start | bytes 2359300
  45.9 0.9 copy-start.10
  47.7 1.7 copy-start.1
  49.4 1.4 copy-start.7
  50.8 11.8 %copy-start.4 = (bf16[1,128,768]{2,1,0:T(8,128)(2,1)S(1)}, bf16[1,128,768]{2,1,0:T(8,128)(2,1)}, u32[]{:S(2)}) copy-start(bf16[1,128,768]{2,1,0:T(8,128)(2,1)} %param.8) | copy-start | bytes 589828
  75.7 2.2 %copy-start.17 = (bf16[4,128,768]{2,1,0:T(8,128)(2,1)S(1)}, bf16[4,128,768]{2,1,0:T(8,128)(2,1)}, u32[]{:S(2)}) copy-start(bf16[4,128,768]{2,1,0:T(8,128)(2,1)} %get-tuple-element.28) | copy-start | bytes 2359300
  77.9 1.8 copy-start.13
  79.7 1.7 copy-start.5
  105.9 14.1 %copy-start.6 = (f32[3,512,64]{1,2,0:T(8,128)S(1)}, f32[3,512,64]{1,2,0:T(8,128)}, u32[]{:S(2)}) copy-start(f32[3,512,64]{1,2,0:T(8,128)} %get-tuple-element.75) | copy-start | bytes 1179652
  116.1 4.0 %copy-start.2 = (f32[3,512,512]{1,2,0:T(8,128)S(1)}, f32[3,512,512]{1,2,0:T(8,128)}, u32[]{:S(2)}) copy-start(f32[3,512,512]{1,2,0:T(8,128)} %copy-done.1) | copy-start | bytes 9437188
  122.5 0.9 copy-start.9
  122.5 1.0 copy-start.11
  123.0 1.2 copy-start.12
  124.2 1.7 copy-start.16
  201.1 5.8 %copy-start.19 = (bf16[192,768]{1,0:T(8,128)(2,1)S(1)}, bf16[192,768]{1,0:T(8,128)(2,1)}, u32[]{:S(2)}) copy-start(bf16[192,768]{1,0:T(8,128)(2,1)} %get-tuple-element.34) | copy-start | bytes 884740
  201.1 6.6 %copy-start.18 = (bf16[288,768]{1,0:T(8,128)(2,1)S(1)}, bf16[288,768]{1,0:T(8,128)(2,1)}, u32[]{:S(2)}) copy-start(bf16[288,768]{1,0:T(8,128)(2,1)} %get-tuple-element.37) | copy-start | bytes 1327108
  204.9 3.8 %copy-start.15 = (bf16[192,2304]{1,0:T(8,128)(2,1)S(1)}, bf16[192,2304]{1,0:T(8,128)(2,1)}, u32[]{:S(2)}) copy-start(bf16[192,2304]{1,0:T(8,128)(2,1)} %get-tuple-element.33) | copy-start | bytes 2654212
  208.7 1.5 copy-start.14
where the time goes:
time: 212 us
  Pallas kernels  151 us (71%)
  other arithmetic  23.4 us (11%)
  matrix products  21.6 us (10%)
  local copies, waits for them, and re-layouts  14.1 us (7%)
    pallas_call x1, Pallas kernels, sum_over_rep(): pl.pallas_call(functools.partial(sum_kernel, streams, early), out_shape=t...  73.2 us
    pallas_call x3, Pallas kernels, gather(): pl.pallas_call(functools.partial(gather_kernel, len(gathered), tuple(kind...  52.5 us
    pallas_call x2, Pallas kernels, scatter(): pl.pallas_call(functools.partial(scatter_kernel, total), out_shape=tuple(...  25.7 us
    dot_general x4, matrix products, outer_sum(): lax.dot_general(left, right, (((0,), (0,)), ((), ())), preferred_element_...  5.64 us
    dot_general x4, matrix products, times_transposed(): lax.dot_general(left, weight, (((1,), (1,)), ((), ())), preferred_element...  5.59 us
    reduce_sum x3, other arithmetic, layer_norm(): mean_row = jnp.mean(values, axis=-1, keepdims=True)  4.27 us

commit v1 on v0

v1 whole, which is shorter than its diff:
```python
import functools

import jax
import jax.numpy as jnp
import numpy as np
from jax import lax
from jax.experimental import pallas as pl
from jax.experimental.pallas import tpu as pltpu
from jax.sharding import PartitionSpec as P

HEAD_DIM = 64
EPSILON = 1e-05
THETA = 160000.0
SQRT_HALF = 0.7071067811865476
INV_SQRT_TAU = 0.3989422804014327
MESH_ID = pl.DeviceIdType.MESH
LANES = 128
VMEM = pl.BlockSpec(memory_space=pltpu.VMEM)
F32 = jnp.float32
B16 = jnp.bfloat16
SEMAPHORES = 448


def normalize(values):
    mean_row = jnp.mean(values, axis=-1, keepdims=True)
    centred = values - mean_row
    variance = jnp.mean(centred * centred, axis=-1, keepdims=True)
    inverse = lax.rsqrt(variance + EPSILON)
    return (centred * inverse, inverse)


def norm_backward(grad_out, normed, inverse, gain):
    grad_normed = grad_out * gain
    gain_grad = jnp.sum(grad_out * normed, axis=0, keepdims=True)
    first = jnp.mean(grad_normed, axis=-1, keepdims=True)
    second = jnp.mean(grad_normed * normed, axis=-1, keepdims=True)
    return (inverse * (grad_normed - first - normed * second), gain_grad)


def gelu_pair(inner):
    cdf = 0.5 * (1.0 + lax.erf(inner * SQRT_HALF))
    return (inner * cdf, cdf + inner * jnp.exp(-0.5 * inner * inner) * INV_SQRT_TAU)


def dot(left, right):
    return jnp.dot(left, right, preferred_element_type=F32)


def outer_sum(left, right):
    return lax.dot_general(left, right, (((0,), (0,)), ((), ())), preferred_element_type=F32)


def times_transposed(left, right):
    return lax.dot_general(left, right, (((1,), (1,)), ((), ())), preferred_element_type=F32)


def flip(index, bit):
    return index + bit * (1 - 2 * ((index // bit) % 2))


def aligned(start, size, unit=16):
    if not isinstance(start, int):
        start = pl.multiple_of(start, unit)
    return pl.ds(start, size)


def remote(src, dst, sems, axis, target):
    return pltpu.make_async_remote_copy(
        src_ref=src,
        dst_ref=dst,
        send_sem=sems(),
        recv_sem=sems(),
        device_id={axis: target},
        device_id_type=MESH_ID,
    )


class Pool:
    def __init__(self, ref):
        self.ref, self.used = ref, 0

    def __call__(self):
        self.used += 1
        assert self.used <= SEMAPHORES
        return self.ref.at[self.used - 1]


class Place:
    def __init__(self):
        self.me = lax.axis_index("shard")
        self.rep = lax.axis_index("rep")
        self.core = flip(self.me, 1)
        self.chip = flip(self.me, 2)
        self.diagonal = flip(self.core, 2)


class AllGather:
    def __init__(self, place, sems, src, dst, tok, chunks):
        self.far, self.near, self.relays = [], [], []
        self.place, self.sems, self.dst, self.tok, self.chunks = place, sems, dst, tok, chunks
        size = tok // chunks
        for c in range(chunks):
            part = src.at[pl.ds(c * size, size)]
            self.far.append(remote(part, self.rows(place.me, c), sems, "shard", place.chip))
        for c in range(chunks):
            part = src.at[pl.ds(c * size, size)]
            self.near.append(remote(part, self.rows(place.me, c), sems, "shard", place.core))

    def rows(self, block, c):
        size = self.tok // self.chunks
        return self.dst.at[aligned(block * self.tok + c * size, size)]

    def start_far(self):
        for copy in self.far:
            copy.start()

    def start_near(self):
        for copy in self.near:
            copy.start()

    def relay(self, c):
        self.far[c].wait_recv()
        region = self.rows(self.place.chip, c)
        copy = remote(region, region, self.sems, "shard", self.place.core)
        copy.start()
        self.relays.append(copy)

    def relay_all(self):
        for c in range(self.chunks):
            self.relay(c)

    def finish_near(self):
        for copy in self.near:
            copy.wait_recv()

    def finish_far(self):
        for copy in self.relays:
            copy.wait_recv()

    def close(self):
        for copy in self.far + self.near + self.relays:
            copy.wait_send()


class ReduceScatter:
    def __init__(self, place, sems, part, near, outgoing, far, tok, chunks):
        self.place, self.sems, self.part, self.near = place, sems, part, near
        self.outgoing, self.far, self.tok, self.chunks = outgoing, far, tok, chunks
        self.size = tok // chunks
        self.first, self.second, self.third = [], [], []

    def rows(self, block, c):
        return aligned(block * self.tok + c * self.size, self.size)

    def piece(self, c):
        return pl.ds(c * self.size, self.size)

    def start(self, block, slot, copies):
        for c in range(self.chunks):
            copy = remote(
                self.part.at[self.rows(block, c)],
                self.near.at[slot, self.piece(c)],
                self.sems,
                "shard",
                self.place.core,
            )
            copy.start()
            copies.append(copy)

    def start_far(self):
        self.start(self.place.diagonal, 0, self.first)

    def start_near(self):
        self.start(self.place.core, 1, self.second)

    def forward(self):
        for c in range(self.chunks):
            self.first[c].wait_recv()
            piece = self.piece(c)
            mine = self.part[self.rows(self.place.chip, c)].astype(F32)
            self.outgoing[piece] = (mine + self.near[0, piece].astype(F32)).astype(B16)
            copy = remote(
                self.outgoing.at[piece], self.far.at[piece], self.sems, "shard", self.place.chip
            )
            copy.start()
            self.third.append(copy)

    def result(self):
        for copy in self.second + self.third:
            copy.wait_recv()
        mine = self.part[aligned(self.place.me * self.tok, self.tok)].astype(F32)
        return mine + self.near[1].astype(F32) + self.far[...].astype(F32)

    def close(self):
        for copy in self.first + self.second + self.third:
            copy.wait_send()


class Swap:
    def __init__(self, place, sems, source, packed, dest, kinds, relays):
        self.place, self.sems, self.source = place, sems, source
        self.packed, self.dest, self.kinds, self.relays = packed, dest, kinds, relays
        self.tall = source.shape[0]
        self.share = self.tall >> relays
        columns = dest.shape[1]
        cut = columns // LANES // 2 * LANES
        low = tuple(1 << i for i in range(relays))
        self.parts = []
        for first, size, order in ((0, cut, low), (cut, columns - cut, low[::-1])):
            position = 0
            for level, bit in enumerate(order):
                position = position + ((place.rep // bit) % 2) * (1 << level)
            self.parts.append((pl.ds(first, size), order, position))
        self.shared, self.whole = [], []

    def pack(self):
        blocks, _, columns = self.packed.shape
        size = columns // self.kinds
        for j in range(blocks):
            for kind in range(self.kinds):
                start = (kind * blocks + j) * size
                self.packed[j, :, kind * size : (kind + 1) * size] = self.source[
                    :, start : start + size
                ]

    def start_far(self):
        place = self.place
        for columns, order, position in self.parts:
            first = position * self.share
            for target in (place.chip, place.diagonal):
                copy = remote(
                    self.packed.at[target, aligned(first, self.share), columns],
                    self.dest.at[aligned(place.me * self.tall + first, self.share), columns],
                    self.sems,
                    "shard",
                    target,
                )
                copy.start()
                self.shared.append((target, columns, order, position, [copy]))

    def start_near(self):
        place = self.place
        mine = aligned(place.me * self.tall, self.tall)
        copy = remote(
            self.packed.at[place.core], self.dest.at[mine], self.sems, "shard", place.core
        )
        copy.start()
        self.whole.append(copy)
        self.dest[mine] = self.packed[place.me]

    def relay(self, level):
        if level >= self.relays:
            return
        for target, columns, order, position, copies in self.shared:
            copies[-1].wait_recv()
            length = self.share << level
            first = (position // (1 << level)) * length
            region = self.dest.at[aligned(target * self.tall + first, length), columns]
            copy = remote(region, region, self.sems, "rep", flip(self.place.rep, order[level]))
            copy.start()
            copies.append(copy)

    def finish(self):
        for entry in self.shared:
            entry[-1][-1].wait_recv()
        for copy in self.whole:
            copy.wait_recv()

    def close(self):
        for copy in self.whole:
            copy.wait_send()
        for entry in self.shared:
            for copy in entry[-1]:
                copy.wait_send()


def halves(order, index):
    length = 1 << len(order)
    offset = 0
    plan = []
    for bit in order:
        length //= 2
        side = (index // bit) % 2
        plan.append((bit, offset + side * length, offset + (1 - side) * length, length))
        offset = offset + side * length
    return plan


def streams_of(rows, n_rep):
    tiles = -(-rows // (16 * n_rep))
    low_first = tuple(1 << i for i in range(n_rep.bit_length() - 1))
    orders = (low_first, low_first[1::-1] + low_first[2:])
    first = min(tiles, -(-7 * tiles // 10))
    streams = []
    base = 0
    for share, order in zip((first, tiles - first), orders):
        if share:
            streams.append((base, 16 * share, order))
            base += 16 * share * n_rep
    return streams, base


class RepSum:
    def __init__(self, place, sems, streams, swap, acc, box, res):
        self.place, self.sems, self.streams, self.swap = place, sems, streams, swap
        self.acc, self.box, self.res = acc, box, res
        self.steps = len(streams[0][2])
        self.plans = [halves(order, place.rep) for _, _, order in streams]
        self.started = [[] for _ in streams]
        self.round = 0

    def at(self, ref, i, piece, length, lead=None):
        base, rows, _ = self.streams[i]
        span = aligned(base + piece * rows, length * rows)
        if not self.swap:
            return ref.at[span]
        return ref.at[slice(None) if lead is None else lead, span]

    def begin(self, i, k):
        plan, steps, place, sems = self.plans[i], self.steps, self.place, self.sems
        acc, box, res = self.acc, self.box, self.res
        if k < steps:
            bit, _, sent, length = plan[k]
            source, target = self.at(acc, i, sent, length), self.at(box, i, length, length)
            copies = [remote(source, target, sems, "rep", flip(place.rep, bit))]
        elif k == steps:
            mine = plan[-1][1]
            if not self.swap:
                copies = [
                    pltpu.make_async_copy(
                        self.at(acc, i, mine, 1), self.at(res, i, mine, 1), sems()
                    )
                ]
            else:
                target_block = self.at(res, i, mine, 1, place.me)
                copies = [
                    remote(self.at(acc, i, mine, 1, target), target_block, sems, "shard", target)
                    for target in (place.core, place.chip, place.diagonal)
                ]
                copies.append(
                    pltpu.make_async_copy(
                        self.at(acc, i, mine, 1, place.me), target_block, sems()
                    )
                )
        else:
            bit, kept, _, length = plan[2 * steps - k]
            region = self.at(res, i, kept, length)
            copies = [remote(region, region, sems, "rep", flip(place.rep, bit))]
        for copy in copies:
            copy.start()
        self.started[i].append(copies)

    def finish(self, i, k):
        copies = self.started[i][k]
        if k == self.steps:
            for copy in copies:
                copy.wait()
            return
        copies[0].wait_recv()
        if k > self.steps:
            return
        acc, box = self.acc, self.box
        base, rows, _ = self.streams[i]
        _, kept, _, length = self.plans[i][k]
        blocks = range(acc.shape[0]) if self.swap else (None,)

        @pl.loop(0, length)
        def _(p):
            to = aligned(base + (kept + p) * rows, rows)
            of = aligned(base + (length + p) * rows, rows)
            for block in blocks:
                x, y = ((to,), (of,)) if block is None else ((block, to), (block, of))
                acc[x] = (acc[x].astype(F32) + box[y].astype(F32)).astype(B16)

    def begin_all(self):
        for i in range(len(self.streams)):
            self.begin(i, 0)

    def advance(self):
        k = self.round
        if k > 2 * self.steps:
            return
        for i in range(len(self.streams)):
            self.finish(i, k)
            if k < 2 * self.steps:
                self.begin(i, k + 1)
        self.round += 1

    def done(self):
        return self.round > 2 * self.steps

    def close(self):
        for i in range(len(self.streams)):
            for k in range(2 * self.steps + 1):
                if k != self.steps:
                    self.started[i][k][0].wait_send()


class Total:
    def __init__(self, place, sems, sums, boxes, bits):
        self.place, self.sems, self.sums, self.boxes, self.bits = place, sems, sums, boxes, bits
        self.copies = []

    def begin(self):
        level = len(self.copies)
        axis, bit = self.bits[level]
        index = self.place.me if axis == "shard" else self.place.rep
        copy = remote(
            self.sums.at[level], self.boxes.at[level], self.sems, axis, flip(index, bit)
        )
        copy.start()
        self.copies.append(copy)

    def advance(self):
        level = len(self.copies) - 1
        if level >= len(self.bits):
            return
        self.copies[level].wait_recv()
        self.sums[level + 1] = self.sums[level] + self.boxes[level]
        if level + 1 < len(self.bits):
            self.begin()
        else:
            self.copies.append(None)

    def done(self):
        return len(self.copies) > len(self.bits)

    def close(self):
        for copy in self.copies[:-1]:
            copy.wait_send()


def pack_block(values, target, t):
    rows, columns = values.shape
    full, rest = divmod(columns, LANES)
    values = values.astype(B16)
    for j in range(full):
        target[t, j * rows : (j + 1) * rows] = values[:, j * LANES : (j + 1) * LANES]
    if rest:
        half = rows // 2
        tail = values[:, full * LANES :]
        target[t, full * rows : full * rows + half] = jnp.concatenate(
            [tail[:half], tail[half:]], axis=1
        )


def unpack_block(source, out, t, kinds):
    blocks = source.shape[0]
    rows, width = out.shape
    columns = width // blocks
    size = columns // kinds
    full, rest = divmod(columns, LANES)
    parts = [source[t, j * rows : (j + 1) * rows] for j in range(full)]
    if rest:
        tail = source[t, full * rows : full * rows + rows // 2]
        parts.append(jnp.concatenate([tail[:, :rest], tail[:, rest:]], axis=0))
    block = jnp.concatenate(parts, axis=1).astype(F32)
    for kind in range(kinds):
        start = (kind * blocks + t) * size
        out[:, start : start + size] = block[:, kind * size : (kind + 1) * size]


def pack_rows(values, target):
    rows = values.shape[0]
    values = values.astype(B16)
    for j in range(values.shape[1] // LANES):
        target[j * rows : (j + 1) * rows] = values[:, j * LANES : (j + 1) * LANES]


def unpack_rows(source, out):
    rows = out.shape[0]
    for j in range(out.shape[1] // LANES):
        out[:, j * LANES : (j + 1) * LANES] = source[j * rows : (j + 1) * rows].astype(F32)


def turned(values):
    lane = lax.broadcasted_iota(jnp.int32, values.shape, 1)
    half = HEAD_DIM // 2
    ahead = pltpu.roll(values, LANES - half, 1)
    behind = pltpu.roll(values, half, 1)
    return jnp.where(lane % HEAD_DIM < half, ahead, behind)


def query_scale(tile, part, rows):
    lane = lax.broadcasted_iota(jnp.int32, (rows, LANES), 1) + tile * LANES
    return jnp.where(lane < part, HEAD_DIM ** (-0.5), 1.0)


class Config:
    pass


def layer_kernel(cfg, *refs):
    r = Config()
    r.__dict__.update(zip(cfg.names, refs))
    r.__dict__.update(jax.tree.unflatten(cfg.tree, refs[len(cfg.names) :]))
    tok, width, part, heads, hidden = cfg.tok, cfg.width, cfg.part, cfg.heads, cfg.hidden
    n_shard, count, chunks = cfg.n_shard, cfg.count, cfg.chunks
    place = Place()
    sems = Pool(r.sems)
    me, core, chip, diagonal = place.me, place.core, place.chip, place.diagonal
    rep_bits = [1 << b for b in range(cfg.n_rep.bit_length() - 1)]
    partners = [("shard", core), ("shard", chip), ("shard", diagonal)]
    partners += [("rep", flip(place.rep, bit)) for bit in rep_bits]
    barrier = pltpu.get_barrier_semaphore()
    for axis, target in partners:
        pl.semaphore_signal(barrier, inc=1, device_id={axis: target}, device_id_type=MESH_ID)
    own = aligned(me * tok, tok)
    half = count // 2
    near_start = (me // 2) * half
    far_start = (chip // 2) * half

    qkv = Swap(place, sems, r.qkv, r.pk_qkv, r.w_qkv, 3, cfg.relays)
    win = Swap(place, sems, r.win, r.pk_in, r.w_in, 2, cfg.relays)
    tokens = AllGather(place, sems, r.tokens, r.toks, tok, chunks)
    grads = AllGather(place, sems, r.grad, r.grads, tok, chunks)
    gains = [
        remote(r.gains, r.all_gains.at[me], sems, "shard", target)
        for target in (core, chip, diagonal)
    ]
    qkv.pack()
    pl.semaphore_wait(barrier, len(partners))
    qkv.start_far()
    tokens.start_far()
    for copy in gains:
        copy.start()
    tokens.start_near()
    qkv.start_near()
    r.toks[own] = r.tokens[...]
    r.grads[own] = r.grad[...]
    r.all_gains[me] = r.gains[...]
    win.pack()
    for name, rows in cfg.padding:
        acc = r.acc[name]
        if len(acc.shape) == 3:
            acc[:, rows:] = jnp.zeros((n_shard, acc.shape[1] - rows, LANES), B16)
        else:
            acc[rows:] = jnp.zeros((acc.shape[0] - rows, LANES), B16)
    normed, inverse = normalize(r.tokens[...].astype(F32))
    r.xhat1[...] = normed
    r.inv1[...] = inverse
    r.sums[0] = jnp.zeros((16, LANES), F32)
    for copy in gains:
        copy.wait_recv()
    for t in range(n_shard):
        columns = slice(t * part, (t + 1) * part)
        r.gain1[:, columns] = r.all_gains[t, 0:1].astype(F32)
        r.gain2[:, columns] = r.all_gains[t, 1:2].astype(F32)

    def normalize_half(start):
        @pl.loop(0, half // tok)
        def _(i):
            rows = aligned(start + i * tok, tok)
            values, _ = normalize(r.toks[rows].astype(F32))
            r.h1[rows] = (values * r.gain1[...]).astype(B16)

    tokens.finish_near()
    normalize_half(near_start)
    qkv.relay(0)
    tokens.relay_all()
    qkv.relay(1)
    grads.start_far()
    grads.start_near()
    win.start_far()
    win.start_near()
    tokens.finish_far()
    normalize_half(far_start)
    qkv.finish()

    @pl.loop(0, 2)
    def _(i):
        rows = aligned(i * half, half)
        projected = dot(r.h1[rows], r.w_qkv[...])
        cosine, sine = r.cosine[rows], r.sine[rows]
        for j in range(3 * part // LANES + 1):
            size = min(LANES, 3 * part - j * LANES)
            tile = projected[:, j * LANES : j * LANES + size]
            if (j + 1) * LANES <= 2 * part:
                tile = tile * cosine + turned(tile) * sine
                if j * LANES < part:
                    tile = tile * query_scale(j, part, half)
            tile = tile.astype(B16)
            for k in range(size // HEAD_DIM):
                index = j * (LANES // HEAD_DIM) + k
                r.heads[index, rows] = tile[:, k * HEAD_DIM : (k + 1) * HEAD_DIM]

    win.relay(0)
    grads.relay_all()

    @pl.loop(0, heads)
    def _(h):
        key, value = r.heads[heads + h], r.heads[2 * heads + h]
        for b in range(2):
            rows = pl.ds(b * half, half)
            scores = times_transposed(r.heads[h, rows], key)
            maxima = jnp.max(scores, axis=-1, keepdims=True)
            expo = jnp.exp(scores - maxima)
            total = jnp.sum(expo, axis=-1, keepdims=True)
            probs = (expo * (1.0 / total)).astype(B16)
            r.probs[h, rows] = probs
            r.att_heads[h, rows] = dot(probs, value).astype(B16)

    for h in range(heads):
        r.att[:, h * HEAD_DIM : (h + 1) * HEAD_DIM] = r.att_heads[h]

    def reduce(name):
        return ReduceScatter(
            place, sems, r.parts[name], r.nears[name], r.outgoing[name], r.fars[name], tok, chunks
        )

    def project(start):
        rows = aligned(start, half)
        r.parts["att"][rows] = dot(r.att[rows], r.w_out[...]).astype(B16)

    mixed = reduce("att")
    project(far_start)
    mixed.start_far()
    project(near_start)
    mixed.start_near()
    win.relay(1)
    mixed.forward()
    resid = r.tokens[...].astype(F32) + mixed.result()
    r.resid[...] = resid
    normed, inverse = normalize(resid)
    r.xhat2[...] = normed
    r.inv2[...] = inverse
    scaled = (normed * r.gain2[...]).astype(B16)
    r.h2[own] = scaled
    second = AllGather(place, sems, r.h2.at[own], r.h2, tok, chunks)
    second.start_far()
    second.start_near()
    win.finish()
    grads.finish_near()
    grads.finish_far()

    def feed_forward(start):
        rows = aligned(start, half)
        upper = dot(r.h2[rows], r.w_in[...])
        inner, gate = upper[:, :hidden], upper[:, hidden:]
        value, slope = gelu_pair(inner)
        act = (value * gate).astype(B16)
        r.act[rows] = act
        grad_act = times_transposed(r.grads[rows], r.down[...])
        grad_upper = jnp.concatenate(
            [grad_act * gate * slope, grad_act * value], axis=-1
        ).astype(B16)
        r.gup[rows] = grad_upper
        r.parts["h2"][rows] = times_transposed(grad_upper, r.w_in[...]).astype(B16)
        r.parts["down"][rows] = dot(act, r.down[...]).astype(B16)

    back2, down = reduce("h2"), reduce("down")
    second.finish_near()
    feed_forward(near_start)
    back2.start_near()
    second.relay_all()
    second.finish_far()
    feed_forward(far_start)
    back2.start_far()
    down.start_near()
    down.start_far()

    groups = {}
    for name, streams, swap in cfg.groups:
        groups[name] = RepSum(
            place, sems, streams, swap, r.acc[name], r.box[name], r.res[name]
        )
    active = []

    def launch(name):
        groups[name].begin_all()
        active.append(groups[name])

    def pump():
        for item in active:
            if not item.done():
                item.advance()

    pack_rows(outer_sum(r.act[...], r.grads[...]), r.acc["down"])
    launch("down")
    back2.forward()

    def pack_pairs(left, right, target):
        for i in range(n_shard // 2):
            columns = slice(i * 2 * part, (i + 1) * 2 * part)
            values = outer_sum(left[:, columns], right[...])
            pack_block(values[:part], target, 2 * i)
            pack_block(values[part:], target, 2 * i + 1)

    pack_pairs(r.h2, r.gup, r.acc["in"])
    launch("in")
    grad_h2 = back2.result()
    back, gain_grad = norm_backward(grad_h2, r.xhat2[...], r.inv2[...], r.gain2[...])
    for j in range(width // LANES):
        r.sums[0, 8 + j : 9 + j] = gain_grad[:, j * LANES : (j + 1) * LANES]
    grad_resid = r.grad[...].astype(F32) + back
    r.gres[...] = grad_resid
    r.resid_b[own] = grad_resid.astype(B16)
    third = AllGather(place, sems, r.resid_b.at[own], r.resid_b, tok, chunks)
    third.start_far()
    third.start_near()
    down.forward()
    pump()

    def attention_grad(start):
        rows = aligned(start, half)
        values = times_transposed(r.resid_b[rows], r.w_out[...]).astype(B16)
        for h in range(heads):
            r.gatt[h, rows] = values[:, h * HEAD_DIM : (h + 1) * HEAD_DIM]

    third.finish_near()
    attention_grad(near_start)
    third.relay_all()
    third.finish_far()
    attention_grad(far_start)
    pack_rows(outer_sum(r.att[...], r.resid_b[...]), r.acc["out"])
    launch("out")

    @pl.loop(0, heads)
    def _(h):
        key, value, query = r.heads[heads + h], r.heads[2 * heads + h], r.heads[h]
        grad_value = jnp.zeros((count, HEAD_DIM), F32)
        grad_key = jnp.zeros((count, HEAD_DIM), F32)
        for b in range(2):
            rows = pl.ds(b * half, half)
            grad_head = r.gatt[h, rows]
            probs = r.probs[h, rows]
            attended = r.att_heads[h, rows].astype(F32)
            delta = jnp.sum(grad_head.astype(F32) * attended, axis=-1, keepdims=True)
            grad_value = grad_value + outer_sum(probs, grad_head)
            grad_probs = times_transposed(grad_head, value)
            grad_scores = (probs.astype(F32) * (grad_probs - delta)).astype(B16)
            r.gheads[h, rows] = dot(grad_scores, key)
            grad_key = grad_key + outer_sum(grad_scores, query[b * half : (b + 1) * half])
        r.gheads[heads + h] = grad_key
        r.gheads[2 * heads + h] = grad_value

    pump()
    grad_parts = reduce("h1")

    def project_back(start):
        rows = aligned(start, half)
        cosine, sine = r.cosine[rows], r.sine[rows]
        for j in range(3 * part // LANES + 1):
            size = min(LANES, 3 * part - j * LANES)
            index = j * (LANES // HEAD_DIM)
            tile = jnp.concatenate(
                [r.gheads[index + k, rows] for k in range(size // HEAD_DIM)], axis=-1
            )
            if (j + 1) * LANES <= 2 * part:
                tile = tile * cosine - turned(tile) * sine
                if j * LANES < part:
                    tile = tile * query_scale(j, part, half)
            r.gproj[rows, j * LANES : j * LANES + size] = tile.astype(B16)
        r.parts["h1"][rows] = times_transposed(r.gproj[rows], r.w_qkv[...]).astype(B16)

    project_back(far_start)
    grad_parts.start_far()
    project_back(near_start)
    grad_parts.start_near()
    pack_pairs(r.h1, r.gproj, r.acc["qkv"])
    launch("qkv")
    grad_parts.forward()
    r.o_output[...] = (r.resid[...] + down.result()).astype(B16)
    pump()
    grad_h1 = grad_parts.result()
    back, gain_grad = norm_backward(grad_h1, r.xhat1[...], r.inv1[...], r.gain1[...])
    for j in range(width // LANES):
        r.sums[0, j : j + 1] = gain_grad[:, j * LANES : (j + 1) * LANES]
    small = Total(
        place, sems, r.sums, r.boxes,
        [("shard", 1), ("shard", 2)] + [("rep", bit) for bit in rep_bits],
    )
    small.begin()
    active.append(small)
    r.o_tokens[...] = r.gres[...] + back
    while not all(item.done() for item in active):
        pump()
    total = r.sums[len(small.bits)]
    for out, at in ((r.o_gain1, 0), (r.o_gain2, 8)):
        row = jnp.concatenate(
            [total[at + j : at + j + 1] for j in range(width // LANES)], axis=1
        )
        picked = jnp.zeros((1, part), F32)
        for t in range(n_shard):
            picked = jnp.where(me == t, row[:, t * part : (t + 1) * part], picked)
        out[...] = picked
    unpack_rows(r.res["down"], r.o_down)
    unpack_rows(r.res["out"], r.o_out)
    for t in range(n_shard):
        unpack_block(r.res["in"], r.o_in, t, 2)
        unpack_block(r.res["qkv"], r.o_qkv, t, 3)
    for copy in gains:
        copy.wait_send()
    for item in [qkv, win, tokens, grads, second, third, mixed, back2, down, grad_parts]:
        item.close()
    for item in active:
        item.close()


def rotary_tables(count):
    half = HEAD_DIM // 2
    freq = THETA ** (-np.arange(half, dtype=np.float64) * 2.0 / HEAD_DIM)
    angles = np.arange(count, dtype=np.float64)[:, None] * freq[None, :]
    angles = np.concatenate([angles, angles], axis=-1)
    sign = np.where(np.arange(HEAD_DIM) < half, -1.0, 1.0)
    repeat = LANES // HEAD_DIM
    cosine = np.tile(np.cos(angles), (1, repeat))
    sine = np.tile(np.sin(angles) * sign, (1, repeat))
    return cosine.astype(np.float32), sine.astype(np.float32)


def local(
    n_shard, n_rep, tokens, gain_one, qkv_weight, out_weight, gain_two, in_weight, down_weight,
    grad_output
):
    tok, width = tokens.shape[1:]
    cfg = Config()
    cfg.n_shard, cfg.n_rep, cfg.tok, cfg.width = n_shard, n_rep, tok, width
    cfg.part = part = width // n_shard
    cfg.heads = heads = part // HEAD_DIM
    cfg.hidden = hidden = down_weight.shape[0]
    cfg.count = count = tok * n_shard
    cfg.chunks = 2
    cfg.relays = min(2, n_rep.bit_length() - 1)
    while cfg.relays and part % (16 << cfg.relays):
        cfg.relays -= 1
    cosine, sine = rotary_tables(count)
    ins = dict(
        tokens=tokens.reshape(tok, width),
        gains=jnp.stack([gain_one, gain_two]),
        qkv=qkv_weight,
        w_out=out_weight,
        win=in_weight,
        down=down_weight,
        grad=grad_output.reshape(tok, width),
        cosine=jnp.asarray(cosine),
        sine=jnp.asarray(sine),
    )
    outs = dict(
        o_output=((tok, width), B16),
        o_tokens=((tok, width), F32),
        o_gain1=((1, part), F32),
        o_qkv=((part, 3 * width), F32),
        o_out=((part, width), F32),
        o_gain2=((1, part), F32),
        o_in=((part, 2 * hidden * n_shard), F32),
        o_down=((hidden, width), F32),
    )
    scratch = dict(
        toks=((count, width), B16),
        grads=((count, width), B16),
        all_gains=((n_shard, 2, part), B16),
        gain1=((1, width), F32),
        gain2=((1, width), F32),
        pk_qkv=((n_shard, part, 3 * part), B16),
        w_qkv=((width, 3 * part), B16),
        pk_in=((n_shard, part, 2 * hidden), B16),
        w_in=((width, 2 * hidden), B16),
        h1=((count, width), B16),
        heads=((3 * heads, count, HEAD_DIM), B16),
        probs=((heads, count, count), B16),
        att_heads=((heads, count, HEAD_DIM), B16),
        att=((count, part), B16),
        h2=((count, width), B16),
        act=((count, hidden), B16),
        gup=((count, 2 * hidden), B16),
        resid=((tok, width), F32),
        xhat1=((tok, width), F32),
        inv1=((tok, 1), F32),
        xhat2=((tok, width), F32),
        inv2=((tok, 1), F32),
        gres=((tok, width), F32),
        resid_b=((count, width), B16),
        gatt=((heads, count, HEAD_DIM), B16),
        gheads=((3 * heads, count, HEAD_DIM), F32),
        gproj=((count, 3 * part), B16),
        sums=((n_rep.bit_length() + 2, 16, LANES), F32),
        boxes=((n_rep.bit_length() + 1, 16, LANES), F32),
    )
    exchanges = ("att", "h2", "down", "h1")
    scratch.update(
        parts={name: ((count, width), B16) for name in exchanges},
        nears={name: ((2, tok, width), B16) for name in exchanges},
        outgoing={name: ((tok, width), B16) for name in exchanges},
        fars={name: ((tok, width), B16) for name in exchanges},
    )
    cfg.groups, cfg.padding, padded = [], [], {}
    for name, rows, swap in (
        ("down", hidden * width // LANES, False),
        ("in", part * 2 * hidden // LANES, True),
        ("out", part * width // LANES, False),
        ("qkv", part * 3 * part // LANES, True),
    ):
        streams, tall = streams_of(rows, n_rep)
        cfg.groups.append((name, streams, swap))
        if tall > rows:
            cfg.padding.append((name, rows))
        padded[name] = ((n_shard, tall, LANES) if swap else (tall, LANES), B16)
    scratch.update(acc=padded, box=padded, res=padded)

    def is_entry(item):
        return isinstance(item, tuple)

    spaces = jax.tree.map(lambda entry: pltpu.VMEM(*entry), scratch, is_leaf=is_entry)
    spaces["sems"] = pltpu.SemaphoreType.DMA((SEMAPHORES,))
    spaces, cfg.tree = jax.tree.flatten(spaces)
    cfg.names = list(ins) + list(outs)
    results = pl.pallas_call(
        functools.partial(layer_kernel, cfg),
        out_shape=tuple(jax.ShapeDtypeStruct(*entry) for entry in outs.values()),
        in_specs=[VMEM] * len(ins),
        out_specs=tuple([VMEM] * len(outs)),
        scratch_shapes=spaces,
        compiler_params=pltpu.CompilerParams(
            collective_id=0, has_side_effects=True, vmem_limit_bytes=63 * 1024 * 1024
        ),
    )(*ins.values())
    output, grad_tokens, gain1, grad_qkv, grad_out, gain2, grad_in, grad_down = results
    return (
        output.reshape(1, tok, width),
        grad_tokens.reshape(1, tok, width),
        gain1.reshape(part),
        grad_qkv,
        grad_out,
        gain2.reshape(part),
        grad_in,
        grad_down,
    )


def solution(mesh):
    in_specs = (
        P("rep", "shard", None),
        P("shard"),
        P("shard", None),
        P("shard", None),
        P("shard"),
        P("shard", None),
        P("shard", None),
        P("rep", "shard", None),
    )
    out_specs = (
        P("rep", "shard", None),
        P("rep", "shard", None),
        P("shard"),
        P("shard", None),
        P("shard", None),
        P("shard"),
        P("shard", None),
        P("shard", None),
    )
    body = functools.partial(local, mesh.shape["shard"], mesh.shape["rep"])
    return jax.shard_map(body, mesh=mesh, in_specs=in_specs, out_specs=out_specs, check_vma=False)
```

time: 212 us -> 140 us (0.66)
  Pallas kernels: 151 us -> 126 us
  other arithmetic: 23.4 us -> 0.57 us
  matrix products: 21.6 us -> 0 us
    pallas_call x6 -> x1, Pallas kernels: 151 us -> 126 us  [local(): pl.pallas_call(functools.partial(layer_kernel, cfg), out_shape=tuple((jax...]
    dot_general x18 -> x0, matrix products: 21.6 us -> none  [the longest x4 5.64 us: outer_sum(): lax.dot_general(left, right, (((0,), (0,)), ((), ())), preferred_element_...]
    reduce_sum x10 -> x0, other arithmetic: 10.1 us -> none  [the longest x3 4.27 us: layer_norm(): mean_row = jnp.mean(values, axis=-1, keepdims=True)]
    convert_element_type x11 -> x0, other arithmetic: 9.89 us -> none  [the longest x1 2.1 us: local(): resid_b, = gather(4, (grad_resid.astype(b16),), (), (), n_shard)]
    unnamed x40 -> x16, local copies, waits for them, and re-layouts: 3.05 us -> 11.6 us
    convert_element_type x4 -> x0, local copies, waits for them, and re-layouts: 3.7 us -> none  [the longest x1 2.22 us: local(): grad_in.astype(b16).reshape(n_shard, part, -1)]
    reshape x4 -> x0, local copies, waits for them, and re-layouts: 2.55 us -> none  [the longest x1 1.23 us: local(): gain_one.reshape(1, part)]
    slice x2 -> x0, local copies, waits for them, and re-layouts: 2.54 us -> none  [the longest x1 1.31 us: local(): sum_g1.reshape(-1)[:part]]
where the time goes in v1:
time: 140 us
  Pallas kernels  126 us (90%)
  local copies, waits for them, and re-layouts  13 us (9%)
    pallas_call x1, Pallas kernels, local(): pl.pallas_call(functools.partial(layer_kernel, cfg), out_shape=tuple((jax...  126 us
    unnamed x16, local copies, waits for them, and re-layouts  11.6 us

profile of v1, /device:TPU:0, one launch (start us, length us, event | category | flops | bytes accessed | tf_op | source)
XLA Modules:
  0.0 139.9 jit_solution(8116783809333876633)
XLA Ops:
  0.6 0.7 stack.9
  1.3 0.7 stack.10
  2.0 0.6 pad_maximum_fusion.refs_1_
  2.5 125.7 %shard_map.161 = (bf16[128,768]{1,0:T(8,128)(2,1)}, f32[128,768]{1,0:T(8,128)}, f32[1,192]{1,0:T(1,128)}, f32[192,2304]{1,0:T(8,128)}, f32[192,768]{1,0:T(8,128)...) custom-call(bf16[128,768]{1,0:T(8,128)(2,1)} %bitcast.7, bf16[2,192]{1,0:T(2,128)(2,1)} %pad_maximum_fusion.refs_1_, ...), custom_call_target="tpu_custom_call" | custom-call | tf_op jit(solution)/shard_map/pallas_call | solution.py:908
  128.3 1.6 %copy.26 = bf16[1,128,768]{2,1,0:T(8,128)(2,1)} copy(bf16[1,128,768]{2,1,0:T(8,128)(2,1)} %bitcast.9) | data formatting | bytes 393216
  129.9 1.8 %copy.27 = f32[1,128,768]{2,1,0:T(8,128)} copy(f32[1,128,768]{2,1,0:T(8,128)} %bitcast.6) | data formatting | bytes 786432
  131.6 1.2 copy.28
  132.9 0.0 copy-start.2
  132.9 0.0 copy-start.3
  132.9 0.0 copy-start
  132.9 2.9 %copy.29 = f32[192,2304]{1,0:T(8,128)} copy(f32[192,2304]{1,0:T(8,128)} %get-tuple-element.35) | data formatting | bytes 3538944
  135.8 0.0 copy-done.2
  135.8 0.8 copy.30
  136.6 0.0 copy-done.3
  136.6 0.6 copy.31
  137.2 0.0 copy-done
  137.2 0.0 copy-start.1
  137.2 1.2 copy.32
  138.4 0.6 copy-done.1
  139.0 0.9 copy.33
Async XLA Ops:
  132.9 3.0 %copy-start.2 = (f32[192,768]{1,0:T(8,128)S(1)}, f32[192,768]{1,0:T(8,128)}, u32[]{:S(2)}) copy-start(f32[192,768]{1,0:T(8,128)} %get-tuple-element.36) | copy-start | bytes 1769476
  132.9 3.8 %copy-start.3 = (f32[1,192]{1,0:T(1,128)S(1)}, f32[1,192]{1,0:T(1,128)}, u32[]{:S(2)}) copy-start(f32[1,192]{1,0:T(1,128)} %get-tuple-element.21) | copy-start | bytes 2308
  132.9 4.3 %copy-start = (f32[192,2304]{1,0:T(8,128)S(1)}, f32[192,2304]{1,0:T(8,128)}, u32[]{:S(2)}) copy-start(f32[192,2304]{1,0:T(8,128)} %get-tuple-element.38) | copy-start | bytes 5308420
  137.2 1.8 %copy-start.1 = (f32[288,768]{1,0:T(8,128)S(1)}, f32[288,768]{1,0:T(8,128)}, u32[]{:S(2)}) copy-start(f32[288,768]{1,0:T(8,128)} %get-tuple-element.39) | copy-start | bytes 2654212

commit v2 on v1

--- a/solution.py
+++ b/solution.py
@@ -289,11 +289,12 @@
 def streams_of(rows, n_rep):
     tiles = -(-rows // (16 * n_rep))
     low_first = tuple(1 << i for i in range(n_rep.bit_length() - 1))
-    orders = (low_first, low_first[1::-1] + low_first[2:])
-    first = min(tiles, -(-7 * tiles // 10))
+    second = low_first[1::-1] + low_first[2:]
+    early = -(-5 * tiles // 7)
+    shares = ((-(-early // 2), low_first), (early // 2, low_first), (tiles - early, second))
     streams = []
     base = 0
-    for share, order in zip((first, tiles - first), orders):
+    for share, order in shares:
         if share:
             streams.append((base, 16 * share, order))
             base += 16 * share * n_rep
@@ -301,57 +302,54 @@
 
 
 class RepSum:
-    def __init__(self, place, sems, streams, swap, acc, box, res):
-        self.place, self.sems, self.streams, self.swap = place, sems, streams, swap
+    def __init__(self, place, sems, stream, swap, acc, box, res):
+        self.place, self.sems, self.swap = place, sems, swap
+        self.base, self.rows, order = stream
         self.acc, self.box, self.res = acc, box, res
-        self.steps = len(streams[0][2])
-        self.plans = [halves(order, place.rep) for _, _, order in streams]
-        self.started = [[] for _ in streams]
+        self.steps = len(order)
+        self.plan = halves(order, place.rep)
+        self.started = []
         self.round = 0
 
-    def at(self, ref, i, piece, length, lead=None):
-        base, rows, _ = self.streams[i]
-        span = aligned(base + piece * rows, length * rows)
+    def at(self, ref, piece, length, lead=None):
+        span = aligned(self.base + piece * self.rows, length * self.rows)
         if not self.swap:
             return ref.at[span]
         return ref.at[slice(None) if lead is None else lead, span]
 
-    def begin(self, i, k):
-        plan, steps, place, sems = self.plans[i], self.steps, self.place, self.sems
+    def begin(self):
+        k, plan, steps, place, sems = self.round, self.plan, self.steps, self.place, self.sems
         acc, box, res = self.acc, self.box, self.res
         if k < steps:
             bit, _, sent, length = plan[k]
-            source, target = self.at(acc, i, sent, length), self.at(box, i, length, length)
+            source, target = self.at(acc, sent, length), self.at(box, length, length)
             copies = [remote(source, target, sems, "rep", flip(place.rep, bit))]
         elif k == steps:
             mine = plan[-1][1]
             if not self.swap:
                 copies = [
-                    pltpu.make_async_copy(
-                        self.at(acc, i, mine, 1), self.at(res, i, mine, 1), sems()
-                    )
+                    pltpu.make_async_copy(self.at(acc, mine, 1), self.at(res, mine, 1), sems())
                 ]
             else:
-                target_block = self.at(res, i, mine, 1, place.me)
+                target_block = self.at(res, mine, 1, place.me)
                 copies = [
-                    remote(self.at(acc, i, mine, 1, target), target_block, sems, "shard", target)
+                    remote(self.at(acc, mine, 1, target), target_block, sems, "shard", target)
                     for target in (place.core, place.chip, place.diagonal)
                 ]
                 copies.append(
-                    pltpu.make_async_copy(
-                        self.at(acc, i, mine, 1, place.me), target_block, sems()
-                    )
+                    pltpu.make_async_copy(self.at(acc, mine, 1, place.me), target_block, sems())
                 )
         else:
             bit, kept, _, length = plan[2 * steps - k]
-            region = self.at(res, i, kept, length)
+            region = self.at(res, kept, length)
             copies = [remote(region, region, sems, "rep", flip(place.rep, bit))]
         for copy in copies:
             copy.start()
-        self.started[i].append(copies)
-
-    def finish(self, i, k):
-        copies = self.started[i][k]
+        self.started.append(copies)
+
+    def finish(self):
+        k = self.round
+        copies = self.started[k]
         if k == self.steps:
             for copy in copies:
                 copy.wait()
@@ -359,9 +357,8 @@
         copies[0].wait_recv()
         if k > self.steps:
             return
-        acc, box = self.acc, self.box
-        base, rows, _ = self.streams[i]
-        _, kept, _, length = self.plans[i][k]
+        acc, box, base, rows = self.acc, self.box, self.base, self.rows
+        _, kept, _, length = self.plan[k]
         blocks = range(acc.shape[0]) if self.swap else (None,)
 
         @pl.loop(0, length)
@@ -372,28 +369,19 @@
                 x, y = ((to,), (of,)) if block is None else ((block, to), (block, of))
                 acc[x] = (acc[x].astype(F32) + box[y].astype(F32)).astype(B16)
 
-    def begin_all(self):
-        for i in range(len(self.streams)):
-            self.begin(i, 0)
-
     def advance(self):
-        k = self.round
-        if k > 2 * self.steps:
-            return
-        for i in range(len(self.streams)):
-            self.finish(i, k)
-            if k < 2 * self.steps:
-                self.begin(i, k + 1)
+        self.finish()
         self.round += 1
+        if not self.done():
+            self.begin()
 
     def done(self):
         return self.round > 2 * self.steps
 
     def close(self):
-        for i in range(len(self.streams)):
-            for k in range(2 * self.steps + 1):
-                if k != self.steps:
-                    self.started[i][k][0].wait_send()
+        for k in range(2 * self.steps + 1):
+            if k != self.steps:
+                self.started[k][0].wait_send()
 
 
 class Total:
@@ -493,7 +481,9 @@
 def layer_kernel(cfg, *refs):
     r = Config()
     r.__dict__.update(zip(cfg.names, refs))
-    r.__dict__.update(jax.tree.unflatten(cfg.tree, refs[len(cfg.names) :]))
+    refs = refs[len(cfg.names) :]
+    r.res = dict(zip(cfg.sums, refs))
+    r.__dict__.update(jax.tree.unflatten(cfg.tree, refs[len(cfg.sums) :]))
     tok, width, part, heads, hidden = cfg.tok, cfg.width, cfg.part, cfg.heads, cfg.hidden
     n_shard, count, chunks = cfg.n_shard, cfg.count, cfg.chunks
     place = Place()
@@ -518,12 +508,14 @@
         remote(r.gains, r.all_gains.at[me], sems, "shard", target)
         for target in (core, chip, diagonal)
     ]
+    r.gains[0:1] = r.gain_one[...].reshape(1, part)
+    r.gains[1:2] = r.gain_two[...].reshape(1, part)
     qkv.pack()
     pl.semaphore_wait(barrier, len(partners))
+    for copy in gains:
+        copy.start()
     qkv.start_far()
     tokens.start_far()
-    for copy in gains:
-        copy.start()
     tokens.start_near()
     qkv.start_near()
     r.toks[own] = r.tokens[...]
@@ -557,12 +549,12 @@
     tokens.finish_near()
     normalize_half(near_start)
     qkv.relay(0)
-    tokens.relay_all()
-    qkv.relay(1)
+    win.start_far()
     grads.start_far()
     grads.start_near()
-    win.start_far()
     win.start_near()
+    qkv.relay(1)
+    tokens.relay_all()
     tokens.finish_far()
     normalize_half(far_start)
     qkv.finish()
@@ -584,9 +576,6 @@
                 index = j * (LANES // HEAD_DIM) + k
                 r.heads[index, rows] = tile[:, k * HEAD_DIM : (k + 1) * HEAD_DIM]
 
-    win.relay(0)
-    grads.relay_all()
-
     @pl.loop(0, heads)
     def _(h):
         key, value = r.heads[heads + h], r.heads[2 * heads + h]
@@ -600,6 +589,7 @@
             r.probs[h, rows] = probs
             r.att_heads[h, rows] = dot(probs, value).astype(B16)
 
+    win.relay(0)
     for h in range(heads):
         r.att[:, h * HEAD_DIM : (h + 1) * HEAD_DIM] = r.att_heads[h]
 
@@ -617,6 +607,7 @@
     mixed.start_far()
     project(near_start)
     mixed.start_near()
+    grads.relay_all()
     win.relay(1)
     mixed.forward()
     resid = r.tokens[...].astype(F32) + mixed.result()
@@ -661,14 +652,16 @@
 
     groups = {}
     for name, streams, swap in cfg.groups:
-        groups[name] = RepSum(
-            place, sems, streams, swap, r.acc[name], r.box[name], r.res[name]
-        )
+        groups[name] = [
+            RepSum(place, sems, stream, swap, r.acc[name], r.box[name], r.res[name])
+            for stream in streams
+        ]
     active = []
 
     def launch(name):
-        groups[name].begin_all()
-        active.append(groups[name])
+        for item in groups[name]:
+            item.begin()
+            active.append(item)
 
     def pump():
         for item in active:
@@ -715,8 +708,7 @@
     pack_rows(outer_sum(r.att[...], r.resid_b[...]), r.acc["out"])
     launch("out")
 
-    @pl.loop(0, heads)
-    def _(h):
+    for h in range(heads):
         key, value, query = r.heads[heads + h], r.heads[2 * heads + h], r.heads[h]
         grad_value = jnp.zeros((count, HEAD_DIM), F32)
         grad_key = jnp.zeros((count, HEAD_DIM), F32)
@@ -733,6 +725,8 @@
             grad_key = grad_key + outer_sum(grad_scores, query[b * half : (b + 1) * half])
         r.gheads[heads + h] = grad_key
         r.gheads[2 * heads + h] = grad_value
+        if h == cfg.pump_head:
+            pump()
 
     pump()
     grad_parts = reduce("h1")
@@ -775,26 +769,53 @@
     r.o_tokens[...] = r.gres[...] + back
     while not all(item.done() for item in active):
         pump()
-    total = r.sums[len(small.bits)]
-    for out, at in ((r.o_gain1, 0), (r.o_gain2, 8)):
-        row = jnp.concatenate(
-            [total[at + j : at + j + 1] for j in range(width // LANES)], axis=1
-        )
-        picked = jnp.zeros((1, part), F32)
-        for t in range(n_shard):
-            picked = jnp.where(me == t, row[:, t * part : (t + 1) * part], picked)
-        out[...] = picked
-    unpack_rows(r.res["down"], r.o_down)
-    unpack_rows(r.res["out"], r.o_out)
-    for t in range(n_shard):
-        unpack_block(r.res["in"], r.o_in, t, 2)
-        unpack_block(r.res["qkv"], r.o_qkv, t, 3)
+    r.o_total[...] = r.sums[len(small.bits)]
     for copy in gains:
         copy.wait_send()
     for item in [qkv, win, tokens, grads, second, third, mixed, back2, down, grad_parts]:
         item.close()
     for item in active:
         item.close()
+
+
+def finish_kernel(cfg, *refs):
+    ins, outs = refs[:7], refs[7:15]
+    stage_qkv, stage_out, stage_in, stage_down, sems = refs[15:]
+    output, grad_tokens, total, res_down, res_in, res_out, res_qkv = ins
+    o_output, o_tokens, o_gain1, o_qkv, o_out, o_gain2, o_in, o_down = outs
+    copies = []
+
+    def send(source, target, pieces):
+        size = source.shape[0] // pieces
+        for i in range(pieces):
+            rows = pl.ds(i * size, size)
+            copy = pltpu.make_async_copy(source.at[rows], target.at[rows], sems.at[len(copies)])
+            copy.start()
+            copies.append(copy)
+
+    send(output, o_output, 1)
+    send(grad_tokens, o_tokens, 1)
+    for t in range(cfg.n_shard):
+        unpack_block(res_qkv, stage_qkv, t, 3)
+    send(stage_qkv, o_qkv, 4)
+    for t in range(cfg.n_shard):
+        unpack_block(res_in, stage_in, t, 2)
+    send(stage_in, o_in, 4)
+    unpack_rows(res_down, stage_down)
+    send(stage_down, o_down, 2)
+    unpack_rows(res_out, stage_out)
+    send(stage_out, o_out, 2)
+    me = lax.axis_index("shard")
+    for out, at in ((o_gain1, 0), (o_gain2, 8)):
+        row = jnp.concatenate(
+            [total[at + j : at + j + 1] for j in range(cfg.width // LANES)], axis=1
+        )
+        picked = jnp.zeros((1, cfg.part), F32)
+        for t in range(cfg.n_shard):
+            picked = jnp.where(me == t, row[:, t * cfg.part : (t + 1) * cfg.part], picked)
+        out[...] = picked
+    for copy in copies:
+        copy.wait()
 
 
 def rotary_tables(count):
@@ -821,13 +842,17 @@
     cfg.hidden = hidden = down_weight.shape[0]
     cfg.count = count = tok * n_shard
     cfg.chunks = 2
+    cfg.pump_head = 1
+    cfg.limit = 44 * 1024 * 1024
+    cfg.finish_limit = 16 * 1024 * 1024
     cfg.relays = min(2, n_rep.bit_length() - 1)
     while cfg.relays and part % (16 << cfg.relays):
         cfg.relays -= 1
     cosine, sine = rotary_tables(count)
     ins = dict(
         tokens=tokens.reshape(tok, width),
-        gains=jnp.stack([gain_one, gain_two]),
+        gain_one=gain_one,
+        gain_two=gain_two,
         qkv=qkv_weight,
         w_out=out_weight,
         win=in_weight,
@@ -837,6 +862,11 @@
         sine=jnp.asarray(sine),
     )
     outs = dict(
+        o_output=((tok, width), B16),
+        o_tokens=((tok, width), F32),
+        o_total=((16, LANES), F32),
+    )
+    results = dict(
         o_output=((tok, width), B16),
         o_tokens=((tok, width), F32),
         o_gain1=((1, part), F32),
@@ -849,6 +879,7 @@
     scratch = dict(
         toks=((count, width), B16),
         grads=((count, width), B16),
+        gains=((2, part), B16),
         all_gains=((n_shard, 2, part), B16),
         gain1=((1, width), F32),
         gain2=((1, width), F32),
@@ -896,7 +927,9 @@
         if tall > rows:
             cfg.padding.append((name, rows))
         padded[name] = ((n_shard, tall, LANES) if swap else (tall, LANES), B16)
-    scratch.update(acc=padded, box=padded, res=padded)
+    scratch.update(acc=padded, box=padded)
+    plain = list(ins) + list(outs)
+    outs.update(padded)
 
     def is_entry(item):
         return isinstance(item, tuple)
@@ -904,17 +937,29 @@
     spaces = jax.tree.map(lambda entry: pltpu.VMEM(*entry), scratch, is_leaf=is_entry)
     spaces["sems"] = pltpu.SemaphoreType.DMA((SEMAPHORES,))
     spaces, cfg.tree = jax.tree.flatten(spaces)
-    cfg.names = list(ins) + list(outs)
-    results = pl.pallas_call(
+    cfg.names, cfg.sums = plain, list(padded)
+    middle = pl.pallas_call(
         functools.partial(layer_kernel, cfg),
         out_shape=tuple(jax.ShapeDtypeStruct(*entry) for entry in outs.values()),
         in_specs=[VMEM] * len(ins),
         out_specs=tuple([VMEM] * len(outs)),
         scratch_shapes=spaces,
         compiler_params=pltpu.CompilerParams(
-            collective_id=0, has_side_effects=True, vmem_limit_bytes=63 * 1024 * 1024
+            collective_id=0, has_side_effects=True, vmem_limit_bytes=cfg.limit
         ),
     )(*ins.values())
+    anywhere = pl.BlockSpec(memory_space=pl.ANY)
+    results = pl.pallas_call(
+        functools.partial(finish_kernel, cfg),
+        out_shape=tuple(jax.ShapeDtypeStruct(*entry) for entry in results.values()),
+        in_specs=[VMEM] * len(middle),
+        out_specs=tuple(VMEM if "gain" in name else anywhere for name in results),
+        scratch_shapes=[
+            pltpu.VMEM(*results[name]) for name in ("o_qkv", "o_out", "o_in", "o_down")
+        ]
+        + [pltpu.SemaphoreType.DMA((16,))],
+        compiler_params=pltpu.CompilerParams(vmem_limit_bytes=cfg.finish_limit),
+    )(*middle)
     output, grad_tokens, gain1, grad_qkv, grad_out, gain2, grad_in, grad_down = results
     return (
         output.reshape(1, tok, width),

time: 140 us -> 129 us (0.921)
  Pallas kernels: 126 us -> 118 us
  local copies, waits for them, and re-layouts: 13 us -> 9.36 us
    pallas_call x1, Pallas kernels: 126 us -> 115 us  [local(): pl.pallas_call(functools.partial(layer_kernel, cfg), out_shape=tuple((jax...]
    pallas_call x0 -> x1, Pallas kernels: none -> 3.61 us  [local(): pl.pallas_call(functools.partial(finish_kernel, cfg), out_shape=tuple((ja...]
    unnamed x16 -> x20, local copies, waits for them, and re-layouts: 11.6 us -> 9.36 us
where the time goes in v2:
time: 129 us; the launch traced here: 128 us
  Pallas kernels  118 us (91%)
  local copies, waits for them, and re-layouts  9.36 us (7%)
    pallas_call x1, Pallas kernels, local(): pl.pallas_call(functools.partial(layer_kernel, cfg), out_shape=tuple((jax...  115 us
    unnamed x20, local copies, waits for them, and re-layouts  9.36 us
    pallas_call x1, Pallas kernels, local(): pl.pallas_call(functools.partial(finish_kernel, cfg), out_shape=tuple((ja...  3.61 us

profile of v2, /device:TPU:0, one launch (start us, length us, event | category | flops | bytes accessed | tf_op | source)
XLA Modules:
  0.0 128.1 jit_solution(623440737994154808)
XLA Ops:
  0.6 0.0 copy-start
  0.6 1.2 copy-done
  1.8 0.0 copy-start.1
  1.8 1.2 copy-done.1
  3.0 0.0 copy-start.2
  3.0 1.0 copy-done.2
  4.0 0.0 copy-start.3
  4.0 1.0 copy-done.3
  4.9 0.0 copy-start.4
  5.0 0.9 copy-done.4
  5.9 0.0 copy-start.5
  5.9 0.9 copy-done.5
  6.8 0.0 copy-start.6
  6.9 0.9 copy-done.6
  7.8 0.0 copy-start.7
  7.8 0.9 copy-done.7
  8.7 0.0 copy-start.8
  8.7 0.7 copy-done.8
  9.4 0.0 copy-start.9
  9.4 0.7 copy-done.9
  10.0 114.5 %shard_map.161 = (bf16[128,768]{1,0:T(8,128)(2,1)S(1)}, f32[128,768]{1,0:T(8,128)S(1)}, f32[16,128]{1,0:T(8,128)S(1)}, bf16[1792,128]{1,0:T(8,128)(2,1)S(1)}, bf...) custom-call(bf16[128,768]{1,0:T(8,128)(2,1)S(1)} %bitcast.6, ...), custom_call_target="tpu_custom_call" | custom-call | tf_op jit(solution)/shard_map/pallas_call | solution.py:941
  124.5 3.6 %shard_map.162 = (bf16[128,768]{1,0:T(8,128)(2,1)}, f32[128,768]{1,0:T(8,128)}, f32[1,192]{1,0:T(1,128)}, f32[192,2304]{1,0:T(8,128)}, f32[192,768]{1,0:T(8,128)...) custom-call(bf16[128,768]{1,0:T(8,128)(2,1)S(1)} %get-tuple-element.23.refs_0_, ...), custom_call_target="tpu_custom_call" | custom-call | tf_op jit(solution)/shard_map/pallas_call | solution.py:952
Async XLA Ops:
  0.6 1.2 copy-start
  1.8 1.2 copy-start.1
  3.0 1.0 copy-start.2
  4.0 1.0 copy-start.3
  4.9 0.9 copy-start.4
  5.9 0.9 copy-start.5
  6.8 0.9 copy-start.6
  7.8 0.9 copy-start.7
  8.7 0.7 copy-start.8
  9.4 0.7 copy-start.9

commit v3 on v2

--- a/solution.py
+++ b/solution.py
@@ -290,8 +290,9 @@
     tiles = -(-rows // (16 * n_rep))
     low_first = tuple(1 << i for i in range(n_rep.bit_length() - 1))
     second = low_first[1::-1] + low_first[2:]
-    early = -(-5 * tiles // 7)
-    shares = ((-(-early // 2), low_first), (early // 2, low_first), (tiles - early, second))
+    third = low_first[:1] + low_first[2:] + low_first[1:2]
+    quarter = tiles // 4
+    shares = ((tiles // 2, second), (tiles - tiles // 2 - quarter, low_first), (quarter, third))
     streams = []
     base = 0
     for share, order in shares:
@@ -388,6 +389,7 @@
     def __init__(self, place, sems, sums, boxes, bits):
         self.place, self.sems, self.sums, self.boxes, self.bits = place, sems, sums, boxes, bits
         self.copies = []
+        self.round = 0
 
     def begin(self):
         level = len(self.copies)
@@ -480,6 +482,8 @@
 
 def layer_kernel(cfg, *refs):
     r = Config()
+    arguments = dict(zip(cfg.inputs, refs))
+    refs = refs[len(cfg.inputs) :]
     r.__dict__.update(zip(cfg.names, refs))
     refs = refs[len(cfg.names) :]
     r.res = dict(zip(cfg.sums, refs))
@@ -495,6 +499,10 @@
     barrier = pltpu.get_barrier_semaphore()
     for axis, target in partners:
         pl.semaphore_signal(barrier, inc=1, device_id={axis: target}, device_id_type=MESH_ID)
+    loads = {}
+    for name in cfg.inputs:
+        loads[name] = pltpu.make_async_copy(arguments[name], getattr(r, name), sems())
+        loads[name].start()
     own = aligned(me * tok, tok)
     half = count // 2
     near_start = (me // 2) * half
@@ -508,9 +516,14 @@
         remote(r.gains, r.all_gains.at[me], sems, "shard", target)
         for target in (core, chip, diagonal)
     ]
+    loads["gain_one"].wait()
+    loads["gain_two"].wait()
     r.gains[0:1] = r.gain_one[...].reshape(1, part)
     r.gains[1:2] = r.gain_two[...].reshape(1, part)
+    loads["qkv"].wait()
     qkv.pack()
+    for name in ("tokens", "win", "grad"):
+        loads[name].wait()
     pl.semaphore_wait(barrier, len(partners))
     for copy in gains:
         copy.start()
@@ -559,6 +572,8 @@
     normalize_half(far_start)
     qkv.finish()
 
+    loads["cosine"].wait()
+    loads["sine"].wait()
     @pl.loop(0, 2)
     def _(i):
         rows = aligned(i * half, half)
@@ -603,13 +618,15 @@
         r.parts["att"][rows] = dot(r.att[rows], r.w_out[...]).astype(B16)
 
     mixed = reduce("att")
+    loads["w_out"].wait()
+    loads["down"].wait()
     project(far_start)
     mixed.start_far()
     project(near_start)
     mixed.start_near()
+    mixed.forward()
+    win.relay(1)
     grads.relay_all()
-    win.relay(1)
-    mixed.forward()
     resid = r.tokens[...].astype(F32) + mixed.result()
     r.resid[...] = resid
     normed, inverse = normalize(resid)
@@ -663,9 +680,9 @@
             item.begin()
             active.append(item)
 
-    def pump():
-        for item in active:
-            if not item.done():
+    def pump(items=None, least=0):
+        for item in active if items is None else items:
+            if item.round >= least and not item.done():
                 item.advance()
 
     pack_rows(outer_sum(r.act[...], r.grads[...]), r.acc["down"])
@@ -682,6 +699,7 @@
     pack_pairs(r.h2, r.gup, r.acc["in"])
     launch("in")
     grad_h2 = back2.result()
+    pump(groups["down"])
     back, gain_grad = norm_backward(grad_h2, r.xhat2[...], r.inv2[...], r.gain2[...])
     for j in range(width // LANES):
         r.sums[0, 8 + j : 9 + j] = gain_grad[:, j * LANES : (j + 1) * LANES]
@@ -692,7 +710,6 @@
     third.start_far()
     third.start_near()
     down.forward()
-    pump()
 
     def attention_grad(start):
         rows = aligned(start, half)
@@ -703,6 +720,7 @@
     third.finish_near()
     attention_grad(near_start)
     third.relay_all()
+    pump()
     third.finish_far()
     attention_grad(far_start)
     pack_rows(outer_sum(r.att[...], r.resid_b[...]), r.acc["out"])
@@ -725,10 +743,9 @@
             grad_key = grad_key + outer_sum(grad_scores, query[b * half : (b + 1) * half])
         r.gheads[heads + h] = grad_key
         r.gheads[2 * heads + h] = grad_value
-        if h == cfg.pump_head:
+        if h < cfg.pump_heads:
             pump()
 
-    pump()
     grad_parts = reduce("h1")
 
     def project_back(start):
@@ -755,7 +772,7 @@
     launch("qkv")
     grad_parts.forward()
     r.o_output[...] = (r.resid[...] + down.result()).astype(B16)
-    pump()
+    pump(None, 1)
     grad_h1 = grad_parts.result()
     back, gain_grad = norm_backward(grad_h1, r.xhat1[...], r.inv1[...], r.gain1[...])
     for j in range(width // LANES):
@@ -842,7 +859,7 @@
     cfg.hidden = hidden = down_weight.shape[0]
     cfg.count = count = tok * n_shard
     cfg.chunks = 2
-    cfg.pump_head = 1
+    cfg.pump_heads = 2
     cfg.limit = 44 * 1024 * 1024
     cfg.finish_limit = 16 * 1024 * 1024
     cfg.relays = min(2, n_rep.bit_length() - 1)
@@ -850,16 +867,16 @@
         cfg.relays -= 1
     cosine, sine = rotary_tables(count)
     ins = dict(
-        tokens=tokens.reshape(tok, width),
         gain_one=gain_one,
         gain_two=gain_two,
         qkv=qkv_weight,
-        w_out=out_weight,
+        tokens=tokens.reshape(tok, width),
         win=in_weight,
-        down=down_weight,
         grad=grad_output.reshape(tok, width),
         cosine=jnp.asarray(cosine),
         sine=jnp.asarray(sine),
+        w_out=out_weight,
+        down=down_weight,
     )
     outs = dict(
         o_output=((tok, width), B16),
@@ -928,7 +945,8 @@
             cfg.padding.append((name, rows))
         padded[name] = ((n_shard, tall, LANES) if swap else (tall, LANES), B16)
     scratch.update(acc=padded, box=padded)
-    plain = list(ins) + list(outs)
+    scratch.update({name: (value.shape, value.dtype) for name, value in ins.items()})
+    plain = list(outs)
     outs.update(padded)
 
     def is_entry(item):
@@ -937,17 +955,17 @@
     spaces = jax.tree.map(lambda entry: pltpu.VMEM(*entry), scratch, is_leaf=is_entry)
     spaces["sems"] = pltpu.SemaphoreType.DMA((SEMAPHORES,))
     spaces, cfg.tree = jax.tree.flatten(spaces)
-    cfg.names, cfg.sums = plain, list(padded)
+    cfg.inputs, cfg.names, cfg.sums = list(ins), plain, list(padded)
     middle = pl.pallas_call(
         functools.partial(layer_kernel, cfg),
         out_shape=tuple(jax.ShapeDtypeStruct(*entry) for entry in outs.values()),
-        in_specs=[VMEM] * len(ins),
+        in_specs=[pl.BlockSpec(memory_space=pltpu.HBM)] * len(ins),
         out_specs=tuple([VMEM] * len(outs)),
         scratch_shapes=spaces,
         compiler_params=pltpu.CompilerParams(
             collective_id=0, has_side_effects=True, vmem_limit_bytes=cfg.limit
         ),
-    )(*ins.values())
+    )(*[pltpu.with_memory_space_constraint(value, pltpu.HBM) for value in ins.values()])
     anywhere = pl.BlockSpec(memory_space=pl.ANY)
     results = pl.pallas_call(
         functools.partial(finish_kernel, cfg),

time: 129 us -> 119 us (0.922)
  local copies, waits for them, and re-layouts: 9.36 us -> 0 us
    unnamed x20 -> x0, local copies, waits for them, and re-layouts: 9.36 us -> none
where the time goes in v3:
time: 119 us
  Pallas kernels  118 us (99%)
    pallas_call x1, Pallas kernels, local(): pl.pallas_call(functools.partial(layer_kernel, cfg), out_shape=tuple((jax...  114 us
    pallas_call x1, Pallas kernels, local(): pl.pallas_call(functools.partial(finish_kernel, cfg), out_shape=tuple((ja...  3.61 us

profile of v3, /device:TPU:0, one launch (start us, length us, event | category | flops | bytes accessed | tf_op | source)
XLA Modules:
  0.0 118.9 jit_solution(11141131369458124475)
XLA Ops:
  0.6 114.5 %shard_map.161 = (bf16[128,768]{1,0:T(8,128)(2,1)S(1)}, f32[128,768]{1,0:T(8,128)S(1)}, f32[16,128]{1,0:T(8,128)S(1)}, bf16[1792,128]{1,0:T(8,128)(2,1)S(1)}, bf...) custom-call(bf16[192]{0:T(256)(128)(2,1)} %refs_0_.1, ...), custom_call_target="tpu_custom_call" | custom-call | tf_op jit(solution)/shard_map/pallas_call | solution.py:959
  115.1 3.6 %shard_map.162 = (bf16[128,768]{1,0:T(8,128)(2,1)}, f32[128,768]{1,0:T(8,128)}, f32[1,192]{1,0:T(1,128)}, f32[192,2304]{1,0:T(8,128)}, f32[192,768]{1,0:T(8,128)...) custom-call(bf16[128,768]{1,0:T(8,128)(2,1)S(1)} %get-tuple-element.23.refs_0_, ...), custom_call_target="tpu_custom_call" | custom-call | tf_op jit(solution)/shard_map/pallas_call | solution.py:970

commit v4 on v3

--- a/solution.py
+++ b/solution.py
@@ -1,4 +1,5 @@
 import functools
+import heapq
 
 import jax
 import jax.numpy as jnp
@@ -18,7 +19,9 @@
 VMEM = pl.BlockSpec(memory_space=pltpu.VMEM)
 F32 = jnp.float32
 B16 = jnp.bfloat16
-SEMAPHORES = 448
+SEMAPHORES = 576
+HOP_US = 1.9
+LINK_BYTES_PER_US = 90000.0
 
 
 def normalize(values):
@@ -286,20 +289,45 @@
     return plan
 
 
-def streams_of(rows, n_rep):
+def streams_of(rows, n_rep, most):
     tiles = -(-rows // (16 * n_rep))
     low_first = tuple(1 << i for i in range(n_rep.bit_length() - 1))
     second = low_first[1::-1] + low_first[2:]
-    third = low_first[:1] + low_first[2:] + low_first[1:2]
-    quarter = tiles // 4
-    shares = ((tiles // 2, second), (tiles - tiles // 2 - quarter, low_first), (quarter, third))
+    most = min(most, tiles)
     streams = []
     base = 0
-    for share, order in shares:
-        if share:
-            streams.append((base, 16 * share, order))
-            base += 16 * share * n_rep
+    for i in range(most):
+        share = tiles // most + (i < tiles % most)
+        streams.append((base, 16 * share, second if i % 3 == 1 else low_first))
+        base += 16 * share * n_rep
     return streams, base
+
+
+class Schedule:
+    def __init__(self):
+        self.free = {}
+        self.queue = []
+        self.count = 0
+
+    def put(self, item, now):
+        for link, time in item.cost():
+            start = max(now, self.free.get(link, 0.0))
+            self.free[link] = start + time
+        self.count += 1
+        heapq.heappush(self.queue, (start + time + HOP_US, self.count, item))
+
+    def launch(self, items, now):
+        for item in items:
+            item.begin()
+            self.put(item, now)
+
+    def pump(self, now, until=None):
+        until = now if until is None else until
+        while self.queue and self.queue[0][0] <= until:
+            arrival, _, item = heapq.heappop(self.queue)
+            item.advance()
+            if not item.done():
+                self.put(item, max(arrival, now))
 
 
 class RepSum:
@@ -379,6 +407,17 @@
     def done(self):
         return self.round > 2 * self.steps
 
+    def cost(self):
+        k, steps = self.round, self.steps
+        blocks = self.acc.shape[0] if self.swap else 1
+        piece = 2 * self.rows * LANES * 2 * blocks / LINK_BYTES_PER_US
+        if k == steps:
+            return [(-1, piece / 2 if self.swap else 0.0)]
+        bit, _, _, length = self.plan[k if k < steps else 2 * steps - k]
+        if bit > 2:
+            return [(2, piece * length), (bit, 2 * piece * length)]
+        return [(bit, piece * length)]
+
     def close(self):
         for k in range(2 * self.steps + 1):
             if k != self.steps:
@@ -414,6 +453,9 @@
 
     def done(self):
         return len(self.copies) > len(self.bits)
+
+    def cost(self):
+        return [(0, 0.0)]
 
     def close(self):
         for copy in self.copies[:-1]:
@@ -673,20 +715,10 @@
             RepSum(place, sems, stream, swap, r.acc[name], r.box[name], r.res[name])
             for stream in streams
         ]
-    active = []
-
-    def launch(name):
-        for item in groups[name]:
-            item.begin()
-            active.append(item)
-
-    def pump(items=None, least=0):
-        for item in active if items is None else items:
-            if item.round >= least and not item.done():
-                item.advance()
+    plan = Schedule()
 
     pack_rows(outer_sum(r.act[...], r.grads[...]), r.acc["down"])
-    launch("down")
+    plan.launch(groups["down"], 0.0)
     back2.forward()
 
     def pack_pairs(left, right, target):
@@ -697,9 +729,9 @@
             pack_block(values[part:], target, 2 * i + 1)
 
     pack_pairs(r.h2, r.gup, r.acc["in"])
-    launch("in")
+    plan.launch(groups["in"], 1.6)
+    plan.pump(1.6, 5.6)
     grad_h2 = back2.result()
-    pump(groups["down"])
     back, gain_grad = norm_backward(grad_h2, r.xhat2[...], r.inv2[...], r.gain2[...])
     for j in range(width // LANES):
         r.sums[0, 8 + j : 9 + j] = gain_grad[:, j * LANES : (j + 1) * LANES]
@@ -710,6 +742,7 @@
     third.start_far()
     third.start_near()
     down.forward()
+    plan.pump(7.0)
 
     def attention_grad(start):
         rows = aligned(start, half)
@@ -719,12 +752,16 @@
 
     third.finish_near()
     attention_grad(near_start)
-    third.relay_all()
-    pump()
+    plan.pump(8.5, 9.5)
+    third.relay(0)
+    plan.pump(10.5, 11.5)
+    third.relay(1)
+    plan.pump(12.0)
     third.finish_far()
     attention_grad(far_start)
     pack_rows(outer_sum(r.att[...], r.resid_b[...]), r.acc["out"])
-    launch("out")
+    plan.pump(13.5)
+    plan.launch(groups["out"], 13.5)
 
     for h in range(heads):
         key, value, query = r.heads[heads + h], r.heads[2 * heads + h], r.heads[h]
@@ -743,8 +780,7 @@
             grad_key = grad_key + outer_sum(grad_scores, query[b * half : (b + 1) * half])
         r.gheads[heads + h] = grad_key
         r.gheads[2 * heads + h] = grad_value
-        if h < cfg.pump_heads:
-            pump()
+        plan.pump(14.4 + 0.9 * h)
 
     grad_parts = reduce("h1")
 
@@ -768,11 +804,12 @@
     grad_parts.start_far()
     project_back(near_start)
     grad_parts.start_near()
+    plan.pump(17.9)
     pack_pairs(r.h1, r.gproj, r.acc["qkv"])
-    launch("qkv")
+    plan.launch(groups["qkv"], 18.9)
     grad_parts.forward()
     r.o_output[...] = (r.resid[...] + down.result()).astype(B16)
-    pump(None, 1)
+    plan.pump(19.5, 24.0)
     grad_h1 = grad_parts.result()
     back, gain_grad = norm_backward(grad_h1, r.xhat1[...], r.inv1[...], r.gain1[...])
     for j in range(width // LANES):
@@ -781,17 +818,15 @@
         place, sems, r.sums, r.boxes,
         [("shard", 1), ("shard", 2)] + [("rep", bit) for bit in rep_bits],
     )
-    small.begin()
-    active.append(small)
+    plan.launch([small], 25.0)
     r.o_tokens[...] = r.gres[...] + back
-    while not all(item.done() for item in active):
-        pump()
+    plan.pump(25.5, float("inf"))
     r.o_total[...] = r.sums[len(small.bits)]
     for copy in gains:
         copy.wait_send()
     for item in [qkv, win, tokens, grads, second, third, mixed, back2, down, grad_parts]:
         item.close()
-    for item in active:
+    for item in sum(groups.values(), [small]):
         item.close()
 
 
@@ -859,7 +894,6 @@
     cfg.hidden = hidden = down_weight.shape[0]
     cfg.count = count = tok * n_shard
     cfg.chunks = 2
-    cfg.pump_heads = 2
     cfg.limit = 44 * 1024 * 1024
     cfg.finish_limit = 16 * 1024 * 1024
     cfg.relays = min(2, n_rep.bit_length() - 1)
@@ -933,13 +967,13 @@
         fars={name: ((tok, width), B16) for name in exchanges},
     )
     cfg.groups, cfg.padding, padded = [], [], {}
-    for name, rows, swap in (
-        ("down", hidden * width // LANES, False),
-        ("in", part * 2 * hidden // LANES, True),
-        ("out", part * width // LANES, False),
-        ("qkv", part * 3 * part // LANES, True),
+    for name, rows, swap, most in (
+        ("down", hidden * width // LANES, False, 4),
+        ("in", part * 2 * hidden // LANES, True, 7),
+        ("out", part * width // LANES, False, 3),
+        ("qkv", part * 3 * part // LANES, True, 7),
     ):
-        streams, tall = streams_of(rows, n_rep)
+        streams, tall = streams_of(rows, n_rep, most)
         cfg.groups.append((name, streams, swap))
         if tall > rows:
             cfg.padding.append((name, rows))

time: 119 us -> 116 us (0.975)
  Pallas kernels: 118 us -> 115 us
    pallas_call x1, Pallas kernels: 114 us -> 112 us  [local(): pl.pallas_call(functools.partial(layer_kernel, cfg), out_shape=tuple((jax...]
where the time goes in v4:
time: 116 us
  Pallas kernels  115 us (99%)
    pallas_call x1, Pallas kernels, local(): pl.pallas_call(functools.partial(layer_kernel, cfg), out_shape=tuple((jax...  112 us
    pallas_call x1, Pallas kernels, local(): pl.pallas_call(functools.partial(finish_kernel, cfg), out_shape=tuple((ja...  3.61 us

profile of v4, /device:TPU:0, one launch (start us, length us, event | category | flops | bytes accessed | tf_op | source)
XLA Modules:
  0.0 116.3 jit_solution(14693507030141214178)
XLA Ops:
  0.6 111.8 %shard_map.161 = (bf16[128,768]{1,0:T(8,128)(2,1)S(1)}, f32[128,768]{1,0:T(8,128)S(1)}, f32[16,128]{1,0:T(8,128)S(1)}, bf16[1792,128]{1,0:T(8,128)(2,1)S(1)}, bf...) custom-call(bf16[192]{0:T(256)(128)(2,1)} %refs_0_.1, ...), custom_call_target="tpu_custom_call" | custom-call | tf_op jit(solution)/shard_map/pallas_call | solution.py:993
  112.5 3.6 %shard_map.162 = (bf16[128,768]{1,0:T(8,128)(2,1)}, f32[128,768]{1,0:T(8,128)}, f32[1,192]{1,0:T(1,128)}, f32[192,2304]{1,0:T(8,128)}, f32[192,768]{1,0:T(8,128)...) custom-call(bf16[128,768]{1,0:T(8,128)(2,1)S(1)} %get-tuple-element.23.refs_0_, ...), custom_call_target="tpu_custom_call" | custom-call | tf_op jit(solution)/shard_map/pallas_call | solution.py:1004

commit v5 on v4

--- a/solution.py
+++ b/solution.py
@@ -19,7 +19,7 @@
 VMEM = pl.BlockSpec(memory_space=pltpu.VMEM)
 F32 = jnp.float32
 B16 = jnp.bfloat16
-SEMAPHORES = 576
+SEMAPHORES = 640
 HOP_US = 1.9
 LINK_BYTES_PER_US = 90000.0
 
@@ -289,16 +289,16 @@
     return plan
 
 
-def streams_of(rows, n_rep, most):
+def streams_of(rows, n_rep, pattern):
     tiles = -(-rows // (16 * n_rep))
-    low_first = tuple(1 << i for i in range(n_rep.bit_length() - 1))
-    second = low_first[1::-1] + low_first[2:]
-    most = min(most, tiles)
+    low = tuple(1 << i for i in range(n_rep.bit_length() - 1))
+    orders = {"A": low, "B": low[1::-1] + low[2:], "E": low[:1] + low[2:] + low[1:2]}
+    most = min(len(pattern), tiles)
     streams = []
     base = 0
     for i in range(most):
         share = tiles // most + (i < tiles % most)
-        streams.append((base, 16 * share, second if i % 3 == 1 else low_first))
+        streams.append((base, 16 * share, orders[pattern[i]]))
         base += 16 * share * n_rep
     return streams, base
 
@@ -553,7 +553,7 @@
     qkv = Swap(place, sems, r.qkv, r.pk_qkv, r.w_qkv, 3, cfg.relays)
     win = Swap(place, sems, r.win, r.pk_in, r.w_in, 2, cfg.relays)
     tokens = AllGather(place, sems, r.tokens, r.toks, tok, chunks)
-    grads = AllGather(place, sems, r.grad, r.grads, tok, chunks)
+    grads = AllGather(place, sems, r.grad, r.grads, tok, 2)
     gains = [
         remote(r.gains, r.all_gains.at[me], sems, "shard", target)
         for target in (core, chip, diagonal)
@@ -650,7 +650,7 @@
     for h in range(heads):
         r.att[:, h * HEAD_DIM : (h + 1) * HEAD_DIM] = r.att_heads[h]
 
-    def reduce(name):
+    def reduce(name, chunks=chunks):
         return ReduceScatter(
             place, sems, r.parts[name], r.nears[name], r.outgoing[name], r.fars[name], tok, chunks
         )
@@ -698,7 +698,7 @@
         r.parts["h2"][rows] = times_transposed(grad_upper, r.w_in[...]).astype(B16)
         r.parts["down"][rows] = dot(act, r.down[...]).astype(B16)
 
-    back2, down = reduce("h2"), reduce("down")
+    back2, down = reduce("h2"), reduce("down", 2)
     second.finish_near()
     feed_forward(near_start)
     back2.start_near()
@@ -752,10 +752,10 @@
 
     third.finish_near()
     attention_grad(near_start)
-    plan.pump(8.5, 9.5)
-    third.relay(0)
-    plan.pump(10.5, 11.5)
-    third.relay(1)
+    plan.pump(8.5)
+    for c in range(chunks):
+        third.relay(c)
+        plan.pump(12.5 - 3.6 * (chunks - 1 - c) / chunks)
     plan.pump(12.0)
     third.finish_far()
     attention_grad(far_start)
@@ -893,7 +893,7 @@
     cfg.heads = heads = part // HEAD_DIM
     cfg.hidden = hidden = down_weight.shape[0]
     cfg.count = count = tok * n_shard
-    cfg.chunks = 2
+    cfg.chunks = 4
     cfg.limit = 44 * 1024 * 1024
     cfg.finish_limit = 16 * 1024 * 1024
     cfg.relays = min(2, n_rep.bit_length() - 1)
@@ -967,13 +967,13 @@
         fars={name: ((tok, width), B16) for name in exchanges},
     )
     cfg.groups, cfg.padding, padded = [], [], {}
-    for name, rows, swap, most in (
-        ("down", hidden * width // LANES, False, 4),
-        ("in", part * 2 * hidden // LANES, True, 7),
-        ("out", part * width // LANES, False, 3),
-        ("qkv", part * 3 * part // LANES, True, 7),
+    for name, rows, swap, pattern in (
+        ("down", hidden * width // LANES, False, "EBAA"),
+        ("in", part * 2 * hidden // LANES, True, "ABAAAAA"),
+        ("out", part * width // LANES, False, "AAE"),
+        ("qkv", part * 3 * part // LANES, True, "AAAABAB"),
     ):
-        streams, tall = streams_of(rows, n_rep, most)
+        streams, tall = streams_of(rows, n_rep, pattern)
         cfg.groups.append((name, streams, swap))
         if tall > rows:
             cfg.padding.append((name, rows))

time: 116 us -> 114 us (0.983)
  Pallas kernels: 115 us -> 113 us
    pallas_call x1, Pallas kernels: 112 us -> 110 us  [local(): pl.pallas_call(functools.partial(layer_kernel, cfg), out_shape=tuple((jax...]
where the time goes in v5:
time: 114 us
  Pallas kernels  113 us (99%)
    pallas_call x1, Pallas kernels, local(): pl.pallas_call(functools.partial(layer_kernel, cfg), out_shape=tuple((jax...  110 us
    pallas_call x1, Pallas kernels, local(): pl.pallas_call(functools.partial(finish_kernel, cfg), out_shape=tuple((ja...  3.61 us

profile of v5, /device:TPU:0, one launch (start us, length us, event | category | flops | bytes accessed | tf_op | source)
XLA Modules:
  0.0 114.3 jit_solution(10117436447312233048)
XLA Ops:
  0.6 109.9 %shard_map.161 = (bf16[128,768]{1,0:T(8,128)(2,1)S(1)}, f32[128,768]{1,0:T(8,128)S(1)}, f32[16,128]{1,0:T(8,128)S(1)}, bf16[1792,128]{1,0:T(8,128)(2,1)S(1)}, bf...) custom-call(bf16[192]{0:T(256)(128)(2,1)} %refs_0_.1, ...), custom_call_target="tpu_custom_call" | custom-call | tf_op jit(solution)/shard_map/pallas_call | solution.py:993
  110.5 3.6 %shard_map.162 = (bf16[128,768]{1,0:T(8,128)(2,1)}, f32[128,768]{1,0:T(8,128)}, f32[1,192]{1,0:T(1,128)}, f32[192,2304]{1,0:T(8,128)}, f32[192,768]{1,0:T(8,128)...) custom-call(bf16[128,768]{1,0:T(8,128)(2,1)S(1)} %get-tuple-element.23.refs_0_, ...), custom_call_target="tpu_custom_call" | custom-call | tf_op jit(solution)/shard_map/pallas_call | solution.py:1004
